TPU v7x, 32 devices: a whole 2x2x4 slice. The times are simulated.
32 devices in a mesh: groups: 2 (over y), batch: 8 (over z, x), mp: 2 (over core).
Axes of the slice: x: 2, y: 2, z: 4, core: 2. Of those that a mesh axis runs over, the one named last changes fastest.
Arguments:
- tokens: bfloat16 [1024, 16384], P(('groups', 'batch')), parts along dimension 0, may hold values from -6 to 6
- gate_weight: bfloat16 [16384, 256], P('batch', 'mp'), may hold values from -0.046875 to 0.046875
- up_weight: bfloat16 [16384, 256], P('batch', 'mp'), may hold values from -0.046875 to 0.046875
- down_weight: bfloat16 [256, 16384], P('mp', 'batch'), may hold values from -0.5 to 0.5
Outputs:
- mixed: bfloat16 [1024, 16384], P(('groups', 'batch'), 'mp'), parts along dimension 0
There are 2 independent parts, one for each index of `groups`. A program takes and returns all parts, laid end to end along the dimension named above; an argument that names none is the same for every part. Nothing has to cross between parts.
All inputs are finite; a program needn't handle non-finite values.
Results may differ from a plain program's by a relative error of at most 0.018.
Values may be sent and summed in bfloat16 or wider, within the bound.
No kernel may reach another device: no remote copies, remote signals or barrier semaphores. Data moves between devices by JAX's collectives and lax.ppermute only.
A program may use at most 64 MiB of HBM per device.

v0:
```python
import jax
import jax.numpy as jnp
from jax import lax
from jax.sharding import PartitionSpec as P


def in_order(parts, index):
    if len(parts) == 1:
        return parts
    if len(parts) == 2:
        first, second = parts
        return [jnp.where(index == 0, first, second), jnp.where(index == 0, second, first)]
    stack = jnp.take(jnp.stack(parts), index ^ jnp.arange(len(parts)), axis=0)
    return [stack[k] for k in range(len(parts))]


def per_device(tokens, gate_weight, up_weight, down_weight, *, n_groups, n_batch, n_mp):
    n_row = n_batch // n_mp
    rows = tokens.shape[0]
    block, units = gate_weight.shape
    columns = down_weight.shape[1]
    axes = ("batch", "mp")
    batch = lax.axis_index("batch")
    core = lax.axis_index("mp")
    group = lax.axis_index("groups")
    row = batch // n_mp
    lane = batch % n_mp
    halved = n_groups == 2 and n_mp == 2 and n_row % 2 == 0
    near = n_row // 2 if halved else n_row

    def device(r, a, c):
        return (r * n_mp + a) * n_mp + c

    every = [(r, a, c) for r in range(n_row) for a in range(n_mp) for c in range(n_mp)]

    def swap(value, step):
        return lax.ppermute(
            value, axes, [(device(r, a, c), device(r ^ step, c, a)) for r, a, c in every]
        )

    def give_out(value, step, turn):
        if halved:
            pairs = [(device(r, a, c), device(r ^ step, c, a ^ turn)) for r, a, c in every]
        else:
            pairs = [
                (device(r, a, c), device(((r * n_mp + a) % n_row) ^ step, c, (r * n_mp + a) // n_row))
                for r, a, c in every
            ]
        return lax.ppermute(value, axes, pairs)

    def others(value, axis, size):
        return [
            lax.ppermute(value, axis, [(c, c ^ step) for c in range(size)])
            for step in range(1, size)
        ]

    def cores(value):
        return in_order([value] + others(value, "mp", n_mp), core)

    order = list(range(n_row))[::-1]

    arrived = {}
    for step in order:
        start = ((row ^ step) * n_mp + core) * block
        sent = lax.dynamic_slice_in_dim(tokens, start, block, 1)
        arrived[step] = swap(sent, step)

    weights = cores(gate_weight) + cores(up_weight)
    weights = jnp.concatenate(weights, axis=1)
    downs = [jnp.concatenate(cores(down_weight), axis=0)]
    if halved:
        part = units // 2
        far = lax.dynamic_slice_in_dim(down_weight, group * part, part, 0)
        far = lax.ppermute(far, "batch", [(b, b ^ (near * n_mp)) for b in range(n_batch)])
        fars = in_order([far] + others(far, "groups", 2), group)
        far = jnp.concatenate(fars, axis=0)
        downs.append(jnp.concatenate(cores(far), axis=0))

    total = None
    for step in order[::-1]:
        partial = jnp.dot(arrived[step], weights, preferred_element_type=jnp.float32)
        back = swap(partial.astype(jnp.bfloat16), step)
        back = back.astype(jnp.float32)
        total = back if total is None else total + back
    for part in others(total, "mp", n_mp):
        total = total + part

    gate = total[:, : n_mp * units]
    up = total[:, n_mp * units :]
    hidden = (jax.nn.silu(gate) * up).astype(jnp.bfloat16)

    theirs = []
    for step in range(near):
        theirs.append(swap(hidden, step))
    mixed = jnp.zeros((rows, n_row * columns), jnp.bfloat16)
    if halved:
        stacked = jnp.concatenate(theirs, axis=0)
        both = [
            jnp.dot(stacked, down, preferred_element_type=jnp.float32).astype(jnp.bfloat16)
            for down in downs
        ]
        side = row // near
        for step in range(near)[::-1]:
            for turn in range(2):
                mine, other = (r[step * rows : (step + 1) * rows] for r in both)
                sent = jnp.where(lane ^ turn == side, mine, other)
                got = give_out(sent, step, turn)
                at = ((row % near) ^ step) * n_mp + (core ^ turn)
                mixed = lax.dynamic_update_slice_in_dim(mixed, got, at * columns, 1)
        return mixed
    stacked = jnp.stack(theirs)
    for step in order:
        wanted = row ^ (batch % n_row) ^ step
        hidden_rows = lax.dynamic_index_in_dim(stacked, wanted, 0, keepdims=False)
        result = jnp.dot(hidden_rows, downs[0], preferred_element_type=jnp.float32)
        got = give_out(result.astype(jnp.bfloat16), step, 0)
        mixed = lax.dynamic_update_slice_in_dim(mixed, got, (row ^ step) * columns, 1)
    return mixed


def solution(mesh):
    sizes = {f"n_{axis}": mesh.shape[axis] for axis in ("groups", "batch", "mp")}

    def body(*args):
        return per_device(*args, **sizes)

    return jax.shard_map(
        body,
        mesh=mesh,
        in_specs=(
            P(("groups", "batch"), None),
            P("batch", "mp"),
            P("batch", "mp"),
            P("mp", "batch"),
        ),
        out_specs=P(("groups", "batch"), "mp"),
        check_vma=False,
    )
```

profile of v0, /device:TPU:0, one launch (start us, length us, event | category | flops | bytes accessed | tf_op | source)
XLA Modules:
  0.0 88.0 jit_solution(12256988384400321975)
XLA Ops:
  0.0 0.6 collective-permute-start.1
  0.6 2.1 %constant_dynamic-slice_fusion.4 = (bf16[64,2048]{1,0:T(8,128)(2,1)}, bf16[64,2048]{1,0:T(8,128)(2,1)}, bf16[64,2048]{1,0:T(8,128)(2,1)S(1)}, bf16[64,2048]{1,0:T(8,128)(2,1)}) fusion(bf16[64,16384]{1,0:T(8,128)(2,1)} %param.4, s32[]{:T(128)S(6)} %select_n.127, s32[]{:T(128)S(6)} %select_n.133, s32[]{:T(128)S(6)} %select_n.135, s32[]{:T(128)S(6)} %select_n.134), kind=kLoop, calls=%fused_computation.41 | loop fusion | bytes 2097168 | tf_op jit(solution)/shard_map/dynamic_slice | solution.py:65
  2.6 3.6 %collective-permute-start = (bf16[64,2048]{1,0:T(8,128)(2,1)}, bf16[64,2048]{1,0:T(8,128)(2,1)}, u32[]{:S(2)}, u32[]{:S(2)}) collective-permute-start(bf16[64,2048]{1,0:T(8,128)(2,1)} %get-tuple-element.5), channel_id=1, source_target_pairs={{0,0},{1,2},{2,1},{3,3},{4,4},{5,6},{6,5},{7,7},{8,8},{9,10},{10,9... | collective-permute-start | bytes 786440 | tf_op jit(solution)/shard_map/ppermute | solution.py:37
  6.2 0.0 copy-done.3
  6.2 1.1 %collective-permute-start.2 = (bf16[2048,128]{1,0:T(8,128)(2,1)S(1)}, bf16[2048,128]{1,0:T(8,128)(2,1)S(1)}, u32[]{:S(2)}, u32[]{:S(2)}) collective-permute-start(bf16[2048,128]{1,0:T(8,128)(2,1)S(1)} %copy-done.3), channel_id=1, source_target_pairs={{0,1},{1,0},{2,3},{3,2},{4,5},{5,4},{6,7},{7,6},{8,9},{9,8},{10,11... | collective-permute-start | bytes 1572872 | tf_op jit(solution)/shard_map/ppermute | solution.py:53
  7.4 1.6 %collective-permute-start.4 = (bf16[64,2048]{1,0:T(8,128)(2,1)}, bf16[64,2048]{1,0:T(8,128)(2,1)}, u32[]{:S(2)}, u32[]{:S(2)}) collective-permute-start(bf16[64,2048]{1,0:T(8,128)(2,1)} %get-tuple-element.6), channel_id=1, source_target_pairs={{0,4},{1,6},{2,5},{3,7},{4,0},{5,2},{6,1},{7,3},{8,12},{9,14},{10,... | collective-permute-start | bytes 786440 | tf_op jit(solution)/shard_map/ppermute | solution.py:37
  9.0 0.0 copy-done
  9.0 1.4 %collective-permute-start.13 = (bf16[128,2048]{1,0:T(8,128)(2,1)S(1)}, bf16[128,2048]{1,0:T(8,128)(2,1)S(1)}, u32[]{:S(2)}, u32[]{:S(2)}) collective-permute-start(bf16[128,2048]{1,0:T(8,128)(2,1)S(1)} %copy-done), channel_id=1, source_target_pairs={{0,1},{1,0},{2,3},{3,2},{4,5},{5,4},{6,7},{7,6},{8,9},{9,8},{10,11... | collective-permute-start | bytes 1572872 | tf_op jit(solution)/shard_map/ppermute | solution.py:53
  10.3 0.7 constant_dynamic-slice_fusion
  11.1 0.0 collective-permute-done.1
  11.1 2.6 %collective-permute-start.6 = (bf16[64,2048]{1,0:T(8,128)(2,1)}, bf16[64,2048]{1,0:T(8,128)(2,1)S(1)}, u32[]{:S(2)}, u32[]{:S(2)}) collective-permute-start(bf16[64,2048]{1,0:T(8,128)(2,1)} %get-tuple-element.8), channel_id=1, source_target_pairs={{0,8},{1,10},{2,9},{3,11},{4,12},{5,14},{6,13},{7,15},{8,0},{9,2},... | collective-permute-start | bytes 786440 | tf_op jit(solution)/shard_map/ppermute | solution.py:37
  13.7 0.0 copy-done.2
  13.7 0.1 broadcast_select_fusion.7
  13.7 0.0 collective-permute-done.2
  13.8 0.0 copy-done.4
  13.8 0.8 collective-permute-start.14
  14.6 0.1 broadcast_select_fusion.5
  14.7 0.2 pad_maximum_fusion
  14.9 0.0 collective-permute-done
  14.9 2.1 %collective-permute-start.8 = (bf16[64,2048]{1,0:T(8,128)(2,1)S(1)}, bf16[64,2048]{1,0:T(8,128)(2,1)S(1)}, u32[]{:S(2)}, u32[]{:S(2)}) collective-permute-start(bf16[64,2048]{1,0:T(8,128)(2,1)S(1)} %get-tuple-element.7), channel_id=1, source_target_pairs={{0,12},{1,14},{2,13},{3,15},{4,8},{5,10},{6,9},{7,11},{8,4},{9,6},... | collective-permute-start | bytes 786440 | tf_op jit(solution)/shard_map/ppermute | solution.py:37
  17.0 26.8 %collective-permute-done.14 = bf16[64,2048]{1,0:T(8,128)(2,1)S(1)} collective-permute-done((bf16[64,2048]{1,0:T(8,128)(2,1)S(1)}, bf16[64,2048]{1,0:T(8,128)(2,1)S(1)}, u32[]{:S(2)}, u32[]{:S(2)}) %collective-permute-start.14) | collective-permute-done | bytes 262176 | tf_op jit(solution)/shard_map/ppermute | solution.py:74
  43.9 1.5 %collective-permute-start.15 = (bf16[64,2048]{1,0:T(8,128)(2,1)S(1)}, bf16[64,2048]{1,0:T(8,128)(2,1)S(1)}, u32[]{:S(2)}, u32[]{:S(2)}) collective-permute-start(bf16[64,2048]{1,0:T(8,128)(2,1)S(1)} %collective-permute-done.14), channel_id=1, source_target_pairs={{0,16},{16,0},{1,17},{17,1},{2,18},{18,2},{3,19},{19,3},{4,20},{20... | collective-permute-start | bytes 786440 | tf_op jit(solution)/shard_map/ppermute | solution.py:53
  45.4 1.4 %convolution_convert_fusion.5 = bf16[64,512]{1,0:T(8,128)(2,1)S(1)} fusion(bf16[64,2048]{1,0:T(8,128)(2,1)} %collective-permute-done, bf16[2048,512]{1,0:T(8,128)(2,1)S(1)} %pad_maximum_fusion), kind=kOutput, calls=%fused_computation.6 | convolution fusion | flops 134250496 | bytes 2424832 | tf_op jit(solution)/shard_map/dot_general | solution.py:81
  46.8 0.0 collective-permute-done.4
  46.8 0.7 collective-permute-start.3
  47.5 1.4 %convolution_convert_fusion.4 = bf16[64,512]{1,0:T(8,128)(2,1)S(1)} fusion(bf16[64,2048]{1,0:T(8,128)(2,1)} %collective-permute-done.4, bf16[2048,512]{1,0:T(8,128)(2,1)S(1)} %pad_maximum_fusion), kind=kOutput, calls=%fused_computation.5 | convolution fusion | flops 134250496 | bytes 2424832 | tf_op jit(solution)/shard_map/dot_general | solution.py:81
  48.9 0.0 collective-permute-done.6
  49.0 0.1 collective-permute-start.5
  49.0 0.5 convolution_convert_fusion.3
  49.5 0.0 collective-permute-done.8
  49.5 3.1 %collective-permute-start.7 = (bf16[64,512]{1,0:T(8,128)(2,1)S(1)}, bf16[64,512]{1,0:T(8,128)(2,1)S(1)}, u32[]{:S(2)}, u32[]{:S(2)}) collective-permute-start(bf16[64,512]{1,0:T(8,128)(2,1)S(1)} %convolution_convert_fusion.3), channel_id=1, source_target_pairs={{0,8},{1,10},{2,9},{3,11},{4,12},{5,14},{6,13},{7,15},{8,0},{9,2},... | collective-permute-start | bytes 196616 | tf_op jit(solution)/shard_map/ppermute | solution.py:37
  52.6 0.5 convolution_convert_fusion.2
  53.1 0.0 collective-permute-done.15
  53.1 1.4 %collective-permute-start.9 = (bf16[64,512]{1,0:T(8,128)(2,1)S(1)}, bf16[64,512]{1,0:T(8,128)(2,1)S(1)}, u32[]{:S(2)}, u32[]{:S(2)}) collective-permute-start(bf16[64,512]{1,0:T(8,128)(2,1)S(1)} %convolution_convert_fusion.2), channel_id=1, source_target_pairs={{0,12},{1,14},{2,13},{3,15},{4,8},{5,10},{6,9},{7,11},{8,4},{9,6},... | collective-permute-start | bytes 196616 | tf_op jit(solution)/shard_map/ppermute | solution.py:37
  54.6 0.0 collective-permute-done.3
  54.6 0.0 collective-permute-done.5
  54.6 0.4 collective-permute-done.7
  55.0 4.4 %collective-permute-done.9 = bf16[64,512]{1,0:T(8,128)(2,1)S(1)} collective-permute-done((bf16[64,512]{1,0:T(8,128)(2,1)S(1)}, bf16[64,512]{1,0:T(8,128)(2,1)S(1)}, u32[]{:S(2)}, u32[]{:S(2)}) %collective-permute-start.9) | collective-permute-done | bytes 65568 | tf_op jit(solution)/shard_map/ppermute | solution.py:37
  59.4 3.3 %collective-permute-start.10 = (f32[64,512]{1,0:T(8,128)S(1)}, f32[64,512]{1,0:T(8,128)S(1)}, u32[]{:S(2)}, u32[]{:S(2)}) collective-permute-start(f32[64,512]{1,0:T(8,128)S(1)} %convert_add_fusion), channel_id=1, source_target_pairs={{0,1},{1,0},{2,3},{3,2},{4,5},{5,4},{6,7},{7,6},{8,9},{9,8},{10,11... | collective-permute-start | bytes 393224 | tf_op jit(solution)/shard_map/ppermute | solution.py:53
  62.7 0.1 collective-permute-start.16
  62.8 0.9 collective-permute-done.10
  63.7 0.7 collective-permute-start.11
  64.4 0.0 collective-permute-done.13
  64.4 0.1 broadcast_select_fusion.3
  64.5 0.1 collective-permute-start.12
  64.5 0.0 collective-permute-done.11
  64.6 3.9 %collective-permute-done.12 = bf16[64,256]{1,0:T(8,128)(2,1)S(1)} collective-permute-done((bf16[64,256]{1,0:T(8,128)(2,1)S(1)}, bf16[64,256]{1,0:T(8,128)(2,1)S(1)}, u32[]{:S(2)}, u32[]{:S(2)}) %collective-permute-start.12) | collective-permute-done | bytes 32800 | tf_op jit(solution)/shard_map/ppermute | solution.py:37
  68.5 0.3 convolution_convert_fusion.1
  68.8 0.0 collective-permute-done.16
  68.8 0.2 broadcast_select_fusion.1
  69.0 0.3 convolution_convert_fusion
  69.3 0.1 broadcast_select_fusion.8
  69.4 0.1 collective-permute-start.17
  69.5 4.7 %collective-permute-start.18 = (bf16[64,2048]{1,0:T(8,128)(2,1)S(1)}, bf16[64,2048]{1,0:T(8,128)(2,1)S(1)}, u32[]{:S(2)}, u32[]{:S(2)}) collective-permute-start(bf16[64,2048]{1,0:T(8,128)(2,1)S(1)} %get-tuple-element.12), channel_id=1, source_target_pairs={{0,5},{1,7},{2,4},{3,6},{4,1},{5,3},{6,0},{7,2},{8,13},{9,15},{10,... | collective-permute-start | bytes 786440 | tf_op jit(solution)/shard_map/ppermute | solution.py:49
  74.2 0.7 collective-permute-start.19
  74.9 0.3 collective-permute-start.20
  75.2 1.0 %collective-permute-done.17 = bf16[64,2048]{1,0:T(8,128)(2,1)S(1)} collective-permute-done((bf16[64,2048]{1,0:T(8,128)(2,1)S(1)}, bf16[64,2048]{1,0:T(8,128)(2,1)S(1)}, u32[]{:S(2)}, u32[]{:S(2)}) %collective-permute-start.17) | collective-permute-done | bytes 262176 | tf_op jit(solution)/shard_map/ppermute | solution.py:49
  76.2 0.1 broadcast_in_dim.3
  76.4 7.7 %collective-permute-done.18 = bf16[64,2048]{1,0:T(8,128)(2,1)S(1)} collective-permute-done((bf16[64,2048]{1,0:T(8,128)(2,1)S(1)}, bf16[64,2048]{1,0:T(8,128)(2,1)S(1)}, u32[]{:S(2)}, u32[]{:S(2)}) %collective-permute-start.18) | collective-permute-done | bytes 262176 | tf_op jit(solution)/shard_map/ppermute | solution.py:49
  84.1 0.0 collective-permute-done.19
  84.1 0.0 copy-start.1
  84.1 3.2 %collective-permute-done.20 = bf16[64,2048]{1,0:T(8,128)(2,1)S(1)} collective-permute-done((bf16[64,2048]{1,0:T(8,128)(2,1)S(1)}, bf16[64,2048]{1,0:T(8,128)(2,1)S(1)}, u32[]{:S(2)}, u32[]{:S(2)}) %collective-permute-start.20) | collective-permute-done | bytes 262176 | tf_op jit(solution)/shard_map/ppermute | solution.py:49
  87.3 0.0 copy-done.1
  87.3 0.7 constant_dynamic-update-slice_fusion.2
  (14 shorter events, 0.2 us)
Async XLA Ops:
  0.0 13.7 %copy-start.2 = (bf16[2048,128]{1,0:T(8,128)(2,1)S(1)}, bf16[2048,128]{1,0:T(8,128)(2,1)}, u32[]{:S(2)}) copy-start(bf16[2048,128]{1,0:T(8,128)(2,1)} %param.5) | copy-start | bytes 1572868
  0.0 6.2 %copy-start.3 = (bf16[2048,128]{1,0:T(8,128)(2,1)S(1)}, bf16[2048,128]{1,0:T(8,128)(2,1)}, u32[]{:S(2)}) copy-start(bf16[2048,128]{1,0:T(8,128)(2,1)} %param.6) | copy-start | bytes 1572868
  0.0 9.0 %copy-start = (bf16[128,2048]{1,0:T(8,128)(2,1)S(1)}, bf16[128,2048]{1,0:T(8,128)(2,1)}, u32[]{:S(2)}) copy-start(bf16[128,2048]{1,0:T(8,128)(2,1)} %param.7) | copy-start | bytes 1572868
  0.0 11.1 %collective-permute-start.1 = (bf16[2048,128]{1,0:T(8,128)(2,1)}, bf16[2048,128]{1,0:T(8,128)(2,1)S(1)}, u32[]{:S(2)}, u32[]{:S(2)}) collective-permute-start(bf16[2048,128]{1,0:T(8,128)(2,1)} %param.5), channel_id=1, source_target_pairs={{0,1},{1,0},{2,3},{3,2},{4,5},{5,4},{6,7},{7,6},{8,9},{9,8},{10,11... | collective-permute-start | bytes 1572872 | tf_op jit(solution)/shard_map/ppermute | solution.py:53
  2.6 12.3 %collective-permute-start = (bf16[64,2048]{1,0:T(8,128)(2,1)}, bf16[64,2048]{1,0:T(8,128)(2,1)}, u32[]{:S(2)}, u32[]{:S(2)}) collective-permute-start(bf16[64,2048]{1,0:T(8,128)(2,1)} %get-tuple-element.5), channel_id=1, source_target_pairs={{0,0},{1,2},{2,1},{3,3},{4,4},{5,6},{6,5},{7,7},{8,8},{9,10},{10,9... | collective-permute-start | bytes 786440 | tf_op jit(solution)/shard_map/ppermute | solution.py:37
  6.2 7.5 %collective-permute-start.2 = (bf16[2048,128]{1,0:T(8,128)(2,1)S(1)}, bf16[2048,128]{1,0:T(8,128)(2,1)S(1)}, u32[]{:S(2)}, u32[]{:S(2)}) collective-permute-start(bf16[2048,128]{1,0:T(8,128)(2,1)S(1)} %copy-done.3), channel_id=1, source_target_pairs={{0,1},{1,0},{2,3},{3,2},{4,5},{5,4},{6,7},{7,6},{8,9},{9,8},{10,11... | collective-permute-start | bytes 1572872 | tf_op jit(solution)/shard_map/ppermute | solution.py:53
  7.4 39.5 %collective-permute-start.4 = (bf16[64,2048]{1,0:T(8,128)(2,1)}, bf16[64,2048]{1,0:T(8,128)(2,1)}, u32[]{:S(2)}, u32[]{:S(2)}) collective-permute-start(bf16[64,2048]{1,0:T(8,128)(2,1)} %get-tuple-element.6), channel_id=1, source_target_pairs={{0,4},{1,6},{2,5},{3,7},{4,0},{5,2},{6,1},{7,3},{8,12},{9,14},{10,... | collective-permute-start | bytes 786440 | tf_op jit(solution)/shard_map/ppermute | solution.py:37
  9.0 55.4 %collective-permute-start.13 = (bf16[128,2048]{1,0:T(8,128)(2,1)S(1)}, bf16[128,2048]{1,0:T(8,128)(2,1)S(1)}, u32[]{:S(2)}, u32[]{:S(2)}) collective-permute-start(bf16[128,2048]{1,0:T(8,128)(2,1)S(1)} %copy-done), channel_id=1, source_target_pairs={{0,1},{1,0},{2,3},{3,2},{4,5},{5,4},{6,7},{7,6},{8,9},{9,8},{10,11... | collective-permute-start | bytes 1572872 | tf_op jit(solution)/shard_map/ppermute | solution.py:53
  11.1 2.7 %copy-start.4 = (bf16[64,2048]{1,0:T(8,128)(2,1)S(1)}, bf16[64,2048]{1,0:T(8,128)(2,1)}, u32[]{:S(2)}) copy-start(bf16[64,2048]{1,0:T(8,128)(2,1)} %constant_dynamic-slice_fusion) | copy-start | bytes 786436
  11.1 37.9 %collective-permute-start.6 = (bf16[64,2048]{1,0:T(8,128)(2,1)}, bf16[64,2048]{1,0:T(8,128)(2,1)S(1)}, u32[]{:S(2)}, u32[]{:S(2)}) collective-permute-start(bf16[64,2048]{1,0:T(8,128)(2,1)} %get-tuple-element.8), channel_id=1, source_target_pairs={{0,8},{1,10},{2,9},{3,11},{4,12},{5,14},{6,13},{7,15},{8,0},{9,2},... | collective-permute-start | bytes 786440 | tf_op jit(solution)/shard_map/ppermute | solution.py:37
  13.8 30.1 %collective-permute-start.14 = (bf16[64,2048]{1,0:T(8,128)(2,1)S(1)}, bf16[64,2048]{1,0:T(8,128)(2,1)S(1)}, u32[]{:S(2)}, u32[]{:S(2)}) collective-permute-start(bf16[64,2048]{1,0:T(8,128)(2,1)S(1)} %copy-done.4), channel_id=1, source_target_pairs={{0,8},{2,10},{4,12},{6,14},{8,0},{10,2},{12,4},{14,6},{1,9},{3,11}... | collective-permute-start | bytes 786440 | tf_op jit(solution)/shard_map/ppermute | solution.py:74
  14.9 34.6 %collective-permute-start.8 = (bf16[64,2048]{1,0:T(8,128)(2,1)S(1)}, bf16[64,2048]{1,0:T(8,128)(2,1)S(1)}, u32[]{:S(2)}, u32[]{:S(2)}) collective-permute-start(bf16[64,2048]{1,0:T(8,128)(2,1)S(1)} %get-tuple-element.7), channel_id=1, source_target_pairs={{0,12},{1,14},{2,13},{3,15},{4,8},{5,10},{6,9},{7,11},{8,4},{9,6},... | collective-permute-start | bytes 786440 | tf_op jit(solution)/shard_map/ppermute | solution.py:37
  43.9 9.2 %collective-permute-start.15 = (bf16[64,2048]{1,0:T(8,128)(2,1)S(1)}, bf16[64,2048]{1,0:T(8,128)(2,1)S(1)}, u32[]{:S(2)}, u32[]{:S(2)}) collective-permute-start(bf16[64,2048]{1,0:T(8,128)(2,1)S(1)} %collective-permute-done.14), channel_id=1, source_target_pairs={{0,16},{16,0},{1,17},{17,1},{2,18},{18,2},{3,19},{19,3},{4,20},{20... | collective-permute-start | bytes 786440 | tf_op jit(solution)/shard_map/ppermute | solution.py:53
  46.8 7.7 %collective-permute-start.3 = (bf16[64,512]{1,0:T(8,128)(2,1)S(1)}, bf16[64,512]{1,0:T(8,128)(2,1)S(1)}, u32[]{:S(2)}, u32[]{:S(2)}) collective-permute-start(bf16[64,512]{1,0:T(8,128)(2,1)S(1)} %convolution_convert_fusion.5), channel_id=1, source_target_pairs={{0,0},{1,2},{2,1},{3,3},{4,4},{5,6},{6,5},{7,7},{8,8},{9,10},{10,9... | collective-permute-start | bytes 196616 | tf_op jit(solution)/shard_map/ppermute | solution.py:37
  49.0 5.6 %collective-permute-start.5 = (bf16[64,512]{1,0:T(8,128)(2,1)S(1)}, bf16[64,512]{1,0:T(8,128)(2,1)S(1)}, u32[]{:S(2)}, u32[]{:S(2)}) collective-permute-start(bf16[64,512]{1,0:T(8,128)(2,1)S(1)} %convolution_convert_fusion.4), channel_id=1, source_target_pairs={{0,4},{1,6},{2,5},{3,7},{4,0},{5,2},{6,1},{7,3},{8,12},{9,14},{10,... | collective-permute-start | bytes 196616 | tf_op jit(solution)/shard_map/ppermute | solution.py:37
  49.5 5.4 %collective-permute-start.7 = (bf16[64,512]{1,0:T(8,128)(2,1)S(1)}, bf16[64,512]{1,0:T(8,128)(2,1)S(1)}, u32[]{:S(2)}, u32[]{:S(2)}) collective-permute-start(bf16[64,512]{1,0:T(8,128)(2,1)S(1)} %convolution_convert_fusion.3), channel_id=1, source_target_pairs={{0,8},{1,10},{2,9},{3,11},{4,12},{5,14},{6,13},{7,15},{8,0},{9,2},... | collective-permute-start | bytes 196616 | tf_op jit(solution)/shard_map/ppermute | solution.py:37
  53.1 6.2 %collective-permute-start.9 = (bf16[64,512]{1,0:T(8,128)(2,1)S(1)}, bf16[64,512]{1,0:T(8,128)(2,1)S(1)}, u32[]{:S(2)}, u32[]{:S(2)}) collective-permute-start(bf16[64,512]{1,0:T(8,128)(2,1)S(1)} %convolution_convert_fusion.2), channel_id=1, source_target_pairs={{0,12},{1,14},{2,13},{3,15},{4,8},{5,10},{6,9},{7,11},{8,4},{9,6},... | collective-permute-start | bytes 196616 | tf_op jit(solution)/shard_map/ppermute | solution.py:37
  59.4 4.3 %collective-permute-start.10 = (f32[64,512]{1,0:T(8,128)S(1)}, f32[64,512]{1,0:T(8,128)S(1)}, u32[]{:S(2)}, u32[]{:S(2)}) collective-permute-start(f32[64,512]{1,0:T(8,128)S(1)} %convert_add_fusion), channel_id=1, source_target_pairs={{0,1},{1,0},{2,3},{3,2},{4,5},{5,4},{6,7},{7,6},{8,9},{9,8},{10,11... | collective-permute-start | bytes 393224 | tf_op jit(solution)/shard_map/ppermute | solution.py:53
  62.7 6.1 %collective-permute-start.16 = (bf16[128,2048]{1,0:T(8,128)(2,1)S(1)}, bf16[128,2048]{1,0:T(8,128)(2,1)S(1)}, u32[]{:S(2)}, u32[]{:S(2)}) collective-permute-start(bf16[128,2048]{1,0:T(8,128)(2,1)S(1)} %pad_maximum_fusion.1), channel_id=1, source_target_pairs={{0,1},{1,0},{2,3},{3,2},{4,5},{5,4},{6,7},{7,6},{8,9},{9,8},{10,11... | collective-permute-start | bytes 1572872 | tf_op jit(solution)/shard_map/ppermute | solution.py:53
  63.7 0.8 collective-permute-start.11
  64.5 4.0 %collective-permute-start.12 = (bf16[64,256]{1,0:T(8,128)(2,1)S(1)}, bf16[64,256]{1,0:T(8,128)(2,1)S(1)}, u32[]{:S(2)}, u32[]{:S(2)}) collective-permute-start(bf16[64,256]{1,0:T(8,128)(2,1)S(1)} %fusion.6), channel_id=1, source_target_pairs={{0,4},{1,6},{2,5},{3,7},{4,0},{5,2},{6,1},{7,3},{8,12},{9,14},{10,... | collective-permute-start | bytes 98312 | tf_op jit(solution)/shard_map/ppermute | solution.py:37
  69.4 6.8 %collective-permute-start.17 = (bf16[64,2048]{1,0:T(8,128)(2,1)S(1)}, bf16[64,2048]{1,0:T(8,128)(2,1)S(1)}, u32[]{:S(2)}, u32[]{:S(2)}) collective-permute-start(bf16[64,2048]{1,0:T(8,128)(2,1)S(1)} %get-tuple-element.11), channel_id=1, source_target_pairs={{0,4},{1,6},{2,5},{3,7},{4,0},{5,2},{6,1},{7,3},{8,12},{9,14},{10,... | collective-permute-start | bytes 786440 | tf_op jit(solution)/shard_map/ppermute | solution.py:49
  69.5 14.5 %collective-permute-start.18 = (bf16[64,2048]{1,0:T(8,128)(2,1)S(1)}, bf16[64,2048]{1,0:T(8,128)(2,1)S(1)}, u32[]{:S(2)}, u32[]{:S(2)}) collective-permute-start(bf16[64,2048]{1,0:T(8,128)(2,1)S(1)} %get-tuple-element.12), channel_id=1, source_target_pairs={{0,5},{1,7},{2,4},{3,6},{4,1},{5,3},{6,0},{7,2},{8,13},{9,15},{10,... | collective-permute-start | bytes 786440 | tf_op jit(solution)/shard_map/ppermute | solution.py:49
  74.2 9.8 %collective-permute-start.19 = (bf16[64,2048]{1,0:T(8,128)(2,1)S(1)}, bf16[64,2048]{1,0:T(8,128)(2,1)S(1)}, u32[]{:S(2)}, u32[]{:S(2)}) collective-permute-start(bf16[64,2048]{1,0:T(8,128)(2,1)S(1)} %get-tuple-element.10), channel_id=1, source_target_pairs={{0,0},{1,2},{2,1},{3,3},{4,4},{5,6},{6,5},{7,7},{8,8},{9,10},{10,9... | collective-permute-start | bytes 786440 | tf_op jit(solution)/shard_map/ppermute | solution.py:49
  74.9 12.4 %collective-permute-start.20 = (bf16[64,2048]{1,0:T(8,128)(2,1)S(1)}, bf16[64,2048]{1,0:T(8,128)(2,1)S(1)}, u32[]{:S(2)}, u32[]{:S(2)}) collective-permute-start(bf16[64,2048]{1,0:T(8,128)(2,1)S(1)} %get-tuple-element.9), channel_id=1, source_target_pairs={{0,1},{1,3},{2,0},{3,2},{4,5},{5,7},{6,4},{7,6},{8,9},{9,11},{10,8... | collective-permute-start | bytes 786440 | tf_op jit(solution)/shard_map/ppermute | solution.py:49
  84.1 3.2 %copy-start.1 = (bf16[64,8192]{1,0:T(8,128)(2,1)}, bf16[64,8192]{1,0:T(8,128)(2,1)S(1)}, u32[]{:S(2)}) copy-start(bf16[64,8192]{1,0:T(8,128)(2,1)S(1)} %constant_dynamic-update-slice_fusion.3) | copy-start | bytes 3145732
where the time goes:
time: 88.4 us; the launch traced here: 88 us
  waiting for transfers between devices  48.2 us (55%)
  starting transfers between devices  30.5 us (35%)
  matrix products  4.41 us (5%)
  local copies, waits for them, and re-layouts  3.68 us (4%)
  other arithmetic  0.93 us (1%)
    ppermute x1, waiting for transfers between devices, per_device(): lax.ppermute(far, 'batch', [(b, b ^ near * n_mp) for b in range(n_batch)])  26.8 us
    ppermute x10, starting transfers between devices, swap(): lax.ppermute(value, axes, [(device(r, a, c), device(r ^ step, c, a)) for...  15.8 us
    ppermute x4, waiting for transfers between devices, give_out(): return lax.ppermute(value, axes, pairs)  11.9 us
    ppermute x10, waiting for transfers between devices, swap(): lax.ppermute(value, axes, [(device(r, a, c), device(r ^ step, c, a)) for...  8.63 us
    ppermute x6, starting transfers between devices, others(): lax.ppermute(value, axis, [(c, c ^ step) for c in range(size)])  8 us
    ppermute x4, starting transfers between devices, give_out(): return lax.ppermute(value, axes, pairs)  5.78 us
    dot_general x4, matrix products, per_device(): jnp.dot(arrived[step], weights, preferred_element_type=jnp.float32)  3.79 us
    dynamic_slice x1, local copies, waits for them, and re-layouts, per_device(): sent = lax.dynamic_slice_in_dim(tokens, start, block, 1)  2.07 us
  transfers between devices with their start and end apart: 21, of which 8 were waited for; matrix products, arithmetic and copies ran while one was open for 9% of the time, Pallas kernels for 0%

commit v1 on v0

v1 whole, which is shorter than its diff:
```python
import functools

import jax
import jax.numpy as jnp
from jax import lax
from jax.experimental import pallas as pl
from jax.experimental.pallas import tpu as pltpu
from jax.sharding import PartitionSpec as P


def in_order(parts, index):
    if len(parts) == 1:
        return parts
    if len(parts) == 2:
        first, second = parts
        return [jnp.where(index == 0, first, second), jnp.where(index == 0, second, first)]
    stack = jnp.take(jnp.stack(parts), index ^ jnp.arange(len(parts)), axis=0)
    return [stack[k] for k in range(len(parts))]


def cut_kernel(place, tokens, *refs, size):
    slabs, sem = refs[:-1], refs[-1]
    block = slabs[0].shape[1] // 2
    first_row = pl.multiple_of(place[0], size)
    copies = []
    for k in range(2 * len(slabs)):
        column = pl.multiple_of(place[1 + k], block)
        copies.append(
            pltpu.make_async_copy(
                tokens.at[pl.ds(first_row, size), pl.ds(column, block)],
                slabs[k // 2].at[:, pl.ds(k % 2 * block, block)],
                sem.at[k],
            )
        )
    for copy in copies:
        copy.start()
    for copy in copies:
        copy.wait()


def cut(place, tokens, n_slab, size, depth):
    slab = jax.ShapeDtypeStruct((size, depth), tokens.dtype)
    return pl.pallas_call(
        functools.partial(cut_kernel, size=size),
        out_shape=[slab] * n_slab,
        in_specs=[pl.BlockSpec(memory_space=pltpu.SMEM), pl.BlockSpec(memory_space=pltpu.HBM)],
        out_specs=[pl.BlockSpec(memory_space=pltpu.VMEM)] * n_slab,
        scratch_shapes=[pltpu.SemaphoreType.DMA((2 * n_slab,))],
        compiler_params=pltpu.CompilerParams(vmem_limit_bytes=8 * 1024 * 1024),
        name="cut",
    )(place, tokens)


def sums_kernel(*refs, n_slab, n_part):
    slabs, weights = refs[:n_slab], refs[n_slab : n_slab + 2 * n_part * n_part]
    outs = refs[n_slab + len(weights) : -1]
    slab_buf = refs[-1]
    size = slabs[0].shape[0]
    block, units = weights[0].shape
    for k, slab in enumerate(slabs):
        slab_buf[k * size : (k + 1) * size] = slab[...]
    wide = n_part * units
    for kind in range(2):
        total = None
        for part in range(n_part):
            first = (part * 2 + kind) * n_part
            product = jnp.dot(
                slab_buf[:, part * block : (part + 1) * block],
                jnp.concatenate([w[...] for w in weights[first : first + n_part]], axis=1),
                preferred_element_type=jnp.float32,
            )
            total = product if total is None else total + product
        for k, out in enumerate(outs):
            part_of = total[k * size : (k + 1) * size]
            out[:, kind * wide : (kind + 1) * wide] = part_of.astype(out.dtype)


def slab_sums(slabs, weights, n_part):
    n_slab = len(slabs)
    size, depth = slabs[0].shape
    wide = 2 * n_part * weights[0].shape[1]
    kept = jax.ShapeDtypeStruct((size, wide), jnp.float32)
    sent = jax.ShapeDtypeStruct((size, wide), jnp.bfloat16)
    vmem = pl.BlockSpec(memory_space=pltpu.VMEM)
    return pl.pallas_call(
        functools.partial(sums_kernel, n_slab=n_slab, n_part=n_part),
        out_shape=[kept] + [sent] * (n_slab - 1),
        in_specs=[vmem] * (n_slab + len(weights)),
        out_specs=[vmem] * n_slab,
        scratch_shapes=[pltpu.VMEM((n_slab * size, depth), jnp.bfloat16)],
        compiler_params=pltpu.CompilerParams(vmem_limit_bytes=16 * 1024 * 1024),
        name="slab_sums",
    )(*slabs, *weights)


def place_kernel(index, *refs):
    blocks, (out, sem) = refs[:-2], refs[-2:]
    columns = blocks[0].shape[1]
    copies = []
    for k, block in enumerate(blocks):
        to = out.at[:, pl.ds(pl.multiple_of((index[0] ^ k) * columns, columns), columns)]
        copies.append(pltpu.make_async_copy(block, to, sem.at[k]))
    for copy in copies:
        copy.start()
    for copy in copies:
        copy.wait()


def place(index, blocks):
    rows, columns = blocks[0].shape
    vmem = pl.BlockSpec(memory_space=pltpu.VMEM)
    return pl.pallas_call(
        place_kernel,
        out_shape=jax.ShapeDtypeStruct((rows, len(blocks) * columns), blocks[0].dtype),
        in_specs=[pl.BlockSpec(memory_space=pltpu.SMEM)] + [vmem] * len(blocks),
        out_specs=pl.BlockSpec(memory_space=pl.ANY),
        scratch_shapes=[pltpu.SemaphoreType.DMA((len(blocks),))],
        compiler_params=pltpu.CompilerParams(vmem_limit_bytes=8 * 1024 * 1024),
        name="place",
    )(index.reshape(1), *blocks)


def per_device(tokens, gate_weight, up_weight, down_weight, *, n_groups, n_batch, n_mp):
    n_row = n_batch // n_mp
    rows = tokens.shape[0]
    block, units = gate_weight.shape
    columns = down_weight.shape[1]
    axes = ("batch", "mp")
    batch = lax.axis_index("batch")
    core = lax.axis_index("mp")
    group = lax.axis_index("groups")
    row = batch // n_mp
    halved = n_groups == 2 and n_mp == 2 and n_row % 2 == 0
    near = n_row // 2 if halved else n_row

    def device(r, a, c):
        return (r * n_mp + a) * n_mp + c

    every = [(r, a, c) for r in range(n_row) for a in range(n_mp) for c in range(n_mp)]

    def swap(value, step):
        return lax.ppermute(
            value, axes, [(device(r, a, c), device(r ^ step, c, a)) for r, a, c in every]
        )

    def give_out(value, step):
        pairs = [
            (device(r, a, c), device(((r * n_mp + a) % n_row) ^ step, c, (r * n_mp + a) // n_row))
            for r, a, c in every
        ]
        return lax.ppermute(value, axes, pairs)

    def away(value, step):
        return lax.ppermute(value, "batch", [(b, b ^ step) for b in range(n_batch)])

    def others(value, axis, size):
        return [
            lax.ppermute(value, axis, [(c, c ^ step) for c in range(size)])
            for step in range(1, size)
        ]

    def cores(value):
        return in_order([value] + others(value, "mp", n_mp), core)

    def dot(left, right):
        return jnp.dot(left, right, preferred_element_type=jnp.float32)

    def halved_plan():
        size = rows // n_mp
        lane = batch % n_mp

        def weight_of(value):
            beside = away(value, 1)
            return [[value] + others(value, "mp", n_mp), [beside] + others(beside, "mp", n_mp)]

        gates, ups = weight_of(gate_weight), weight_of(up_weight)
        pieces = [piece for k in range(n_mp) for kind in (gates, ups) for piece in kind[k]]
        where = jnp.stack(
            [core * size]
            + [((row ^ s) * n_mp + (lane ^ k)) * block for s in range(n_row) for k in range(n_mp)]
        )
        slabs = list(cut(where, tokens, n_row, size, n_mp * block))
        for step in range(1, n_row):
            slabs[step] = away(slabs[step], step * n_mp)
        total, *sent = slab_sums(slabs, pieces, n_mp)
        for step in range(1, n_row):
            got = away(sent[step - 1], step * n_mp)
            total = total + got.astype(jnp.float32)
        gate = total[:, : n_mp * units]
        up = total[:, n_mp * units :]
        hidden = (jax.nn.silu(gate) * up).astype(jnp.bfloat16)
        hidden = jnp.concatenate(in_order([hidden[:, :units], hidden[:, units:]], core), axis=1)
        hidden = jnp.concatenate(cores(hidden), axis=0)

        side = row // near
        near_down = lax.ppermute(
            down_weight,
            axes,
            [(device(r, a, 1 - r // near), device(r, a, r // near)) for r in range(n_row) for a in range(2)],
        )
        far_down = lax.ppermute(
            down_weight,
            ("groups", "batch", "mp"),
            [
                (
                    g * n_batch * 2 + device(r, a, g),
                    g * n_batch * 2 + device(r ^ near, a, r // near),
                )
                for g in range(2)
                for r in range(n_row)
                for a in range(2)
            ],
        )
        holders = [device(r, a, 1 - r // near) for r in range(n_row) for a in range(2)]
        far_down_other = lax.ppermute(
            far_down,
            ("groups", "batch", "mp"),
            [(g * n_batch * 2 + h, (1 - g) * n_batch * 2 + h) for g in range(2) for h in holders],
        )
        own = core == side
        down = in_order(
            [jnp.where(own, down_weight, far_down), jnp.where(own, near_down, far_down_other)],
            jnp.where(own, core, group),
        )
        peers = range(1, near * n_mp)
        gathered = [hidden] + [away(hidden, k) for k in peers]
        result = dot(jnp.concatenate(gathered, axis=0), jnp.concatenate(down, axis=0))
        result = result.astype(jnp.bfloat16)
        blocks = [result[k * rows : (k + 1) * rows] for k in range(near * n_mp)]
        for k in peers:
            blocks[k] = away(blocks[k], k)
        return place(batch % (near * n_mp), blocks)

    if halved:
        return halved_plan()
    arrived = []
    for step in range(n_row):
        start = ((row ^ step) * n_mp + core) * block
        arrived.append(swap(lax.dynamic_slice_in_dim(tokens, start, block, 1), step))
    weights = cores(gate_weight) + cores(up_weight)
    weights = jnp.concatenate(weights, axis=1)
    down = jnp.concatenate(cores(down_weight), axis=0)
    total = 0.0
    for step in range(n_row):
        partial = dot(arrived[step], weights).astype(jnp.bfloat16)
        total = total + swap(partial, step).astype(jnp.float32)
    for part in others(total, "mp", n_mp):
        total = total + part
    gate = total[:, : n_mp * units]
    up = total[:, n_mp * units :]
    hidden = (jax.nn.silu(gate) * up).astype(jnp.bfloat16)
    stacked = jnp.stack([swap(hidden, step) for step in range(n_row)])
    mixed = jnp.zeros((rows, n_row * columns), jnp.bfloat16)
    for step in range(n_row):
        wanted = row ^ (batch % n_row) ^ step
        hidden_rows = lax.dynamic_index_in_dim(stacked, wanted, 0, keepdims=False)
        got = give_out(dot(hidden_rows, down).astype(jnp.bfloat16), step)
        mixed = lax.dynamic_update_slice_in_dim(mixed, got, (row ^ step) * columns, 1)
    return mixed


def solution(mesh):
    sizes = {f"n_{axis}": mesh.shape[axis] for axis in ("groups", "batch", "mp")}

    def body(*args):
        return per_device(*args, **sizes)

    return jax.shard_map(
        body,
        mesh=mesh,
        in_specs=(
            P(("groups", "batch"), None),
            P("batch", "mp"),
            P("batch", "mp"),
            P("mp", "batch"),
        ),
        out_specs=P(("groups", "batch"), "mp"),
        check_vma=False,
    )
```

time: 88.4 us -> 90.9 us (1.028)
  the two profiles are of different devices: /device:TPU:0 before, /device:TPU:18 now
where the time goes in v1:
time: 90.9 us; the launch traced here: 90.7 us
  waiting for transfers between devices  61.6 us (68%)
  starting transfers between devices  23.7 us (26%)
  Pallas kernels  2.68 us (3%)
  local copies, waits for them, and re-layouts  1.8 us (2%)
    ppermute x14, waiting for transfers between devices, away(): return lax.ppermute(value, 'batch', [(b, b ^ step) for b in range(n_batch)])  44 us
    ppermute x14, starting transfers between devices, away(): return lax.ppermute(value, 'batch', [(b, b ^ step) for b in range(n_batch)])  16.9 us
    ppermute x1, waiting for transfers between devices, halved_plan(): lax.ppermute(down_weight, ('groups', 'batch', 'mp'), [(g * n_batch * 2 +...  9.1 us
    ppermute x1, waiting for transfers between devices, halved_plan(): lax.ppermute(far_down, ('groups', 'batch', 'mp'), [(g * n_batch * 2 + h,...  8.48 us
    ppermute x1, starting transfers between devices, halved_plan(): lax.ppermute(down_weight, axes, [(device(r, a, 1 - r // near), device(r,...  2.42 us
    ppermute x1, starting transfers between devices, halved_plan(): lax.ppermute(down_weight, ('groups', 'batch', 'mp'), [(g * n_batch * 2 +...  1.91 us
    ppermute x1, starting transfers between devices, halved_plan(): lax.ppermute(far_down, ('groups', 'batch', 'mp'), [(g * n_batch * 2 + h,...  1.91 us
  transfers between devices with their start and end apart: 22, of which 11 were waited for; matrix products, arithmetic and copies ran while one was open for 0% of the time, Pallas kernels for 1%

profile of v1, /device:TPU:18, one launch (start us, length us, event | category | flops | bytes accessed | tf_op | source)
XLA Modules:
  0.0 90.7 jit_solution(17129772378767973164)
XLA Ops:
  0.0 0.5 collective-permute-start.5
  0.5 1.5 %collective-permute-start.7 = (bf16[2048,128]{1,0:T(8,128)(2,1)}, bf16[2048,128]{1,0:T(8,128)(2,1)S(1)}, u32[]{:S(2)}, u32[]{:S(2)}) collective-permute-start(bf16[2048,128]{1,0:T(8,128)(2,1)} %refs_6_.1), channel_id=1, source_target_pairs={{0,2},{2,0},{4,6},{6,4},{8,10},{10,8},{12,14},{14,12},{1,3},{3,1},... | collective-permute-start | bytes 1572872 | tf_op jit(solution)/shard_map/ppermute | solution.py:154
  2.0 0.1 stack.39.place
  2.1 0.0 copy-start
  2.1 1.6 %copy-done = bf16[64,16384]{1,0:T(8,128)(2,1)S(1)} copy-done((bf16[64,16384]{1,0:T(8,128)(2,1)S(1)}, bf16[64,16384]{1,0:T(8,128)(2,1)}, u32[]{:S(2)}) %copy-start) | copy-done | bytes 2097176
  3.7 0.0 copy-start.1
  3.7 0.0 copy-start.2
  3.7 1.0 %cut.1 = (bf16[32,4096]{1,0:T(8,128)(2,1)S(1)}, bf16[32,4096]{1,0:T(8,128)(2,1)S(1)}, bf16[32,4096]{1,0:T(8,128)(2,1)S(1)}, bf16[32,4096]{1,0:T(8,128)(2,1)S(1)}) custom-call(s32[9]{0:T(128)S(1)} %stack.39.place, bf16[64,16384]{1,0:T(8,128)(2,1)S(1)} %copy-done), custom_call_target="tpu_custom_call" | custom-call | tf_op jit(solution)/shard_map/cut/pallas_call | solution.py:43
  4.7 1.6 %collective-permute-start = (bf16[32,4096]{1,0:T(8,128)(2,1)S(1)}, bf16[32,4096]{1,0:T(8,128)(2,1)S(1)}, u32[]{:S(2)}, u32[]{:S(2)}) collective-permute-start(bf16[32,4096]{1,0:T(8,128)(2,1)S(1)} %get-tuple-element.14), channel_id=1, source_target_pairs={{0,4},{2,6},{4,0},{6,2},{8,12},{10,14},{12,8},{14,10},{1,5},{3,7},... | collective-permute-start | bytes 786440 | tf_op jit(solution)/shard_map/ppermute | solution.py:154
  6.3 0.3 collective-permute-start.1
  6.7 0.0 copy-done.1
  6.7 0.0 collective-permute-start.3
  6.7 9.0 %collective-permute-done.refs_1_ = bf16[32,4096]{1,0:T(8,128)(2,1)S(1)} collective-permute-done((bf16[32,4096]{1,0:T(8,128)(2,1)S(1)}, bf16[32,4096]{1,0:T(8,128)(2,1)S(1)}, u32[]{:S(2)}, u32[]{:S(2)}) %collective-permute-start) | collective-permute-done | bytes 262176 | tf_op jit(solution)/shard_map/ppermute | solution.py:154
  15.7 0.0 copy-done.2
  15.7 0.0 collective-permute-start.4
  15.7 0.0 collective-permute-done.5.refs_8_
  15.7 0.5 collective-permute-start.6
  16.2 8.9 %collective-permute-done.7.refs_10_ = bf16[2048,128]{1,0:T(8,128)(2,1)S(1)} collective-permute-done((bf16[2048,128]{1,0:T(8,128)(2,1)}, bf16[2048,128]{1,0:T(8,128)(2,1)S(1)}, u32[]{:S(2)}, u32[]{:S(2)}) %collective-permute-start.7) | collective-permute-done | bytes 524320 | tf_op jit(solution)/shard_map/ppermute | solution.py:154
  25.1 0.0 collective-permute-start.8
  25.1 0.0 collective-permute-done.1.refs_2_
  25.1 0.5 collective-permute-start.2
  25.6 13.9 %collective-permute-done.2.refs_3_ = bf16[32,4096]{1,0:T(8,128)(2,1)S(1)} collective-permute-done((bf16[32,4096]{1,0:T(8,128)(2,1)S(1)}, bf16[32,4096]{1,0:T(8,128)(2,1)S(1)}, u32[]{:S(2)}, u32[]{:S(2)}) %collective-permute-start.2) | collective-permute-done | bytes 262176 | tf_op jit(solution)/shard_map/ppermute | solution.py:154
  39.5 0.0 collective-permute-done.3.refs_5_
  39.5 0.0 collective-permute-done.4.refs_7_
  39.5 0.0 collective-permute-done.6.refs_9_
  39.5 0.0 collective-permute-done.8.refs_11_
  39.5 0.0 copy-start.3
  39.5 0.7 slab_sums.1
  40.2 0.1 collective-permute-start.10
  40.3 0.5 collective-permute-start.11
  40.8 3.9 %collective-permute-start.9 = (bf16[32,512]{1,0:T(8,128)(2,1)S(1)}, bf16[32,512]{1,0:T(8,128)(2,1)S(1)}, u32[]{:S(2)}, u32[]{:S(2)}) collective-permute-start(bf16[32,512]{1,0:T(8,128)(2,1)S(1)} %get-tuple-element.18), channel_id=1, source_target_pairs={{0,4},{2,6},{4,0},{6,2},{8,12},{10,14},{12,8},{14,10},{1,5},{3,7},... | collective-permute-start | bytes 98312 | tf_op jit(solution)/shard_map/ppermute | solution.py:154
  44.7 0.0 copy-done.3
  44.7 1.9 %collective-permute-start.16 = (bf16[128,2048]{1,0:T(8,128)(2,1)S(1)}, bf16[128,2048]{1,0:T(8,128)(2,1)S(1)}, u32[]{:S(2)}, u32[]{:S(2)}) collective-permute-start(bf16[128,2048]{1,0:T(8,128)(2,1)S(1)} %copy-done.3), channel_id=1, source_target_pairs={{0,8},{2,10},{4,12},{6,14},{8,1},{10,3},{12,5},{14,7},{17,24},{19,... | collective-permute-start | bytes 1572872 | tf_op jit(solution)/shard_map/ppermute | solution.py:201
  46.6 0.0 collective-permute-done.10
  46.6 0.0 collective-permute-done.11
  46.6 0.3 collective-permute-done.9
  47.0 0.1 collective-permute-start.12
  47.1 2.4 %collective-permute-start.17 = (bf16[128,2048]{1,0:T(8,128)(2,1)S(1)}, bf16[128,2048]{1,0:T(8,128)(2,1)S(1)}, u32[]{:S(2)}, u32[]{:S(2)}) collective-permute-start(bf16[128,2048]{1,0:T(8,128)(2,1)S(1)} %copy-done.3), channel_id=1, source_target_pairs={{1,0},{3,2},{5,4},{7,6},{8,9},{10,11},{12,13},{14,15},{17,16},{19,... | collective-permute-start | bytes 1572872 | tf_op jit(solution)/shard_map/ppermute | solution.py:196
  49.5 9.1 %collective-permute-done.16 = bf16[128,2048]{1,0:T(8,128)(2,1)S(1)} collective-permute-done((bf16[128,2048]{1,0:T(8,128)(2,1)S(1)}, bf16[128,2048]{1,0:T(8,128)(2,1)S(1)}, u32[]{:S(2)}, u32[]{:S(2)}) %collective-permute-start.16) | collective-permute-done | bytes 524320 | tf_op jit(solution)/shard_map/ppermute | solution.py:201
  58.6 1.9 %collective-permute-start.18 = (bf16[128,2048]{1,0:T(8,128)(2,1)S(1)}, bf16[128,2048]{1,0:T(8,128)(2,1)S(1)}, u32[]{:S(2)}, u32[]{:S(2)}) collective-permute-start(bf16[128,2048]{1,0:T(8,128)(2,1)S(1)} %collective-permute-done.16), channel_id=1, source_target_pairs={{1,17},{3,19},{5,21},{7,23},{8,24},{10,26},{12,28},{14,30},{17,1},... | collective-permute-start | bytes 1572872 | tf_op jit(solution)/shard_map/ppermute | solution.py:215
  60.5 0.0 collective-permute-done.12
  60.6 0.6 collective-permute-start.13
  61.2 0.0 collective-permute-done.17
  61.2 8.5 %collective-permute-done.18 = bf16[128,2048]{1,0:T(8,128)(2,1)S(1)} collective-permute-done((bf16[128,2048]{1,0:T(8,128)(2,1)S(1)}, bf16[128,2048]{1,0:T(8,128)(2,1)S(1)}, u32[]{:S(2)}, u32[]{:S(2)}) %collective-permute-start.18) | collective-permute-done | bytes 524320 | tf_op jit(solution)/shard_map/ppermute | solution.py:215
  69.7 0.1 broadcast_select_fusion.3
  69.8 3.8 %collective-permute-start.14 = (bf16[64,256]{1,0:T(8,128)(2,1)S(1)}, bf16[64,256]{1,0:T(8,128)(2,1)S(1)}, u32[]{:S(2)}, u32[]{:S(2)}) collective-permute-start(bf16[64,256]{1,0:T(8,128)(2,1)S(1)} %pad_maximum_fusion), channel_id=1, source_target_pairs={{0,4},{2,6},{4,0},{6,2},{8,12},{10,14},{12,8},{14,10},{1,5},{3,7},... | collective-permute-start | bytes 98312 | tf_op jit(solution)/shard_map/ppermute | solution.py:154
  73.6 0.0 collective-permute-start.15
  73.6 0.0 collective-permute-done.13
  73.6 1.9 %collective-permute-done.14 = bf16[64,256]{1,0:T(8,128)(2,1)S(1)} collective-permute-done((bf16[64,256]{1,0:T(8,128)(2,1)S(1)}, bf16[64,256]{1,0:T(8,128)(2,1)S(1)}, u32[]{:S(2)}, u32[]{:S(2)}) %collective-permute-start.14) | collective-permute-done | bytes 32800 | tf_op jit(solution)/shard_map/ppermute | solution.py:154
  75.5 2.9 %collective-permute-done.15 = bf16[64,256]{1,0:T(8,128)(2,1)S(1)} collective-permute-done((bf16[64,256]{1,0:T(8,128)(2,1)S(1)}, bf16[64,256]{1,0:T(8,128)(2,1)S(1)}, u32[]{:S(2)}, u32[]{:S(2)}) %collective-permute-start.15) | collective-permute-done | bytes 32800 | tf_op jit(solution)/shard_map/ppermute | solution.py:154
  78.4 0.4 convolution_convert_fusion
  78.9 0.1 fusion.5
  79.0 0.6 collective-permute-start.19
  79.5 0.4 collective-permute-start.20
  80.0 2.6 %collective-permute-start.21 = (bf16[64,2048]{1,0:T(8,128)(2,1)S(1)}, bf16[64,2048]{1,0:T(8,128)(2,1)S(1)}, u32[]{:S(2)}, u32[]{:S(2)}) collective-permute-start(bf16[64,2048]{1,0:T(8,128)(2,1)S(1)} %get-tuple-element.27), channel_id=1, source_target_pairs={{0,6},{2,4},{4,2},{6,0},{8,14},{10,12},{12,10},{14,8},{1,7},{3,5},... | collective-permute-start | bytes 786440 | tf_op jit(solution)/shard_map/ppermute | solution.py:154
  82.5 2.9 %collective-permute-done.19.refs_1_ = bf16[64,2048]{1,0:T(8,128)(2,1)S(1)} collective-permute-done((bf16[64,2048]{1,0:T(8,128)(2,1)S(1)}, bf16[64,2048]{1,0:T(8,128)(2,1)S(1)}, u32[]{:S(2)}, u32[]{:S(2)}) %collective-permute-start.19) | collective-permute-done | bytes 262176 | tf_op jit(solution)/shard_map/ppermute | solution.py:154
  85.4 0.5 collective-permute-done.20.refs_2_
  85.9 3.8 %collective-permute-done.21.refs_3_ = bf16[64,2048]{1,0:T(8,128)(2,1)S(1)} collective-permute-done((bf16[64,2048]{1,0:T(8,128)(2,1)S(1)}, bf16[64,2048]{1,0:T(8,128)(2,1)S(1)}, u32[]{:S(2)}, u32[]{:S(2)}) %collective-permute-start.21) | collective-permute-done | bytes 262176 | tf_op jit(solution)/shard_map/ppermute | solution.py:154
  89.7 1.0 %place.1 = bf16[64,8192]{1,0:T(8,128)(2,1)} custom-call(s32[1]{0:T(128)} %bitcast.index, bf16[64,2048]{1,0:T(8,128)(2,1)S(1)} %get-tuple-element.30.refs_0_, bf16[64,2048]{1,0:T(8,128)(2,1)S(1)} %collective-permute-done.19.refs_1_, bf16[64,2048]{1,0:T(8,128)(2,1)S(1)} %collective-permute-done.20.refs_2_, bf16[64,2048]{1,0:T(8,128)(2,1)S(1)} %collective-permute-done.21.refs_3_), custom_call_target="tpu_custom_call" | custom-call | tf_op jit(solution)/shard_map/place/pallas_call | solution.py:112
  (10 shorter events, 0.1 us)
Async XLA Ops:
  0.0 15.7 %collective-permute-start.5 = (bf16[2048,128]{1,0:T(8,128)(2,1)}, bf16[2048,128]{1,0:T(8,128)(2,1)S(1)}, u32[]{:S(2)}, u32[]{:S(2)}) collective-permute-start(bf16[2048,128]{1,0:T(8,128)(2,1)} %refs_4_.1), channel_id=1, source_target_pairs={{0,2},{2,0},{4,6},{6,4},{8,10},{10,8},{12,14},{14,12},{1,3},{3,1},... | collective-permute-start | bytes 1572872 | tf_op jit(solution)/shard_map/ppermute | solution.py:154
  0.5 24.6 %collective-permute-start.7 = (bf16[2048,128]{1,0:T(8,128)(2,1)}, bf16[2048,128]{1,0:T(8,128)(2,1)S(1)}, u32[]{:S(2)}, u32[]{:S(2)}) collective-permute-start(bf16[2048,128]{1,0:T(8,128)(2,1)} %refs_6_.1), channel_id=1, source_target_pairs={{0,2},{2,0},{4,6},{6,4},{8,10},{10,8},{12,14},{14,12},{1,3},{3,1},... | collective-permute-start | bytes 1572872 | tf_op jit(solution)/shard_map/ppermute | solution.py:154
  2.1 1.6 %copy-start = (bf16[64,16384]{1,0:T(8,128)(2,1)S(1)}, bf16[64,16384]{1,0:T(8,128)(2,1)}, u32[]{:S(2)}) copy-start(bf16[64,16384]{1,0:T(8,128)(2,1)} %tokens.1) | copy-start | bytes 6291460
  3.7 3.0 %copy-start.1 = (bf16[2048,128]{1,0:T(8,128)(2,1)S(1)}, bf16[2048,128]{1,0:T(8,128)(2,1)}, u32[]{:S(2)}) copy-start(bf16[2048,128]{1,0:T(8,128)(2,1)} %refs_4_.1) | copy-start | bytes 1572868
  3.7 12.0 %copy-start.2 = (bf16[2048,128]{1,0:T(8,128)(2,1)S(1)}, bf16[2048,128]{1,0:T(8,128)(2,1)}, u32[]{:S(2)}) copy-start(bf16[2048,128]{1,0:T(8,128)(2,1)} %refs_6_.1) | copy-start | bytes 1572868
  4.7 11.0 %collective-permute-start = (bf16[32,4096]{1,0:T(8,128)(2,1)S(1)}, bf16[32,4096]{1,0:T(8,128)(2,1)S(1)}, u32[]{:S(2)}, u32[]{:S(2)}) collective-permute-start(bf16[32,4096]{1,0:T(8,128)(2,1)S(1)} %get-tuple-element.14), channel_id=1, source_target_pairs={{0,4},{2,6},{4,0},{6,2},{8,12},{10,14},{12,8},{14,10},{1,5},{3,7},... | collective-permute-start | bytes 786440 | tf_op jit(solution)/shard_map/ppermute | solution.py:154
  6.3 18.8 %collective-permute-start.1 = (bf16[32,4096]{1,0:T(8,128)(2,1)S(1)}, bf16[32,4096]{1,0:T(8,128)(2,1)S(1)}, u32[]{:S(2)}, u32[]{:S(2)}) collective-permute-start(bf16[32,4096]{1,0:T(8,128)(2,1)S(1)} %get-tuple-element.15), channel_id=1, source_target_pairs={{0,8},{2,10},{4,12},{6,14},{8,0},{10,2},{12,4},{14,6},{1,9},{3,11}... | collective-permute-start | bytes 786440 | tf_op jit(solution)/shard_map/ppermute | solution.py:154
  6.7 32.8 %collective-permute-start.3 = (bf16[2048,128]{1,0:T(8,128)(2,1)S(1)}, bf16[2048,128]{1,0:T(8,128)(2,1)S(1)}, u32[]{:S(2)}, u32[]{:S(2)}) collective-permute-start(bf16[2048,128]{1,0:T(8,128)(2,1)S(1)} %copy-done.1), channel_id=1, source_target_pairs={{0,1},{1,0},{2,3},{3,2},{4,5},{5,4},{6,7},{7,6},{8,9},{9,8},{10,11... | collective-permute-start | bytes 1572872 | tf_op jit(solution)/shard_map/ppermute | solution.py:158
  15.7 23.7 %collective-permute-start.4 = (bf16[2048,128]{1,0:T(8,128)(2,1)S(1)}, bf16[2048,128]{1,0:T(8,128)(2,1)S(1)}, u32[]{:S(2)}, u32[]{:S(2)}) collective-permute-start(bf16[2048,128]{1,0:T(8,128)(2,1)S(1)} %copy-done.2), channel_id=1, source_target_pairs={{0,1},{1,0},{2,3},{3,2},{4,5},{5,4},{6,7},{7,6},{8,9},{9,8},{10,11... | collective-permute-start | bytes 1572872 | tf_op jit(solution)/shard_map/ppermute | solution.py:158
  15.7 23.7 %collective-permute-start.6 = (bf16[2048,128]{1,0:T(8,128)(2,1)S(1)}, bf16[2048,128]{1,0:T(8,128)(2,1)S(1)}, u32[]{:S(2)}, u32[]{:S(2)}) collective-permute-start(bf16[2048,128]{1,0:T(8,128)(2,1)S(1)} %collective-permute-done.5.refs_8_), channel_id=1, source_target_pairs={{0,1},{1,0},{2,3},{3,2},{4,5},{5,4},{6,7},{7,6},{8,9},{9,8},{10,11... | collective-permute-start | bytes 1572872 | tf_op jit(solution)/shard_map/ppermute | solution.py:158
  25.1 14.4 %collective-permute-start.8 = (bf16[2048,128]{1,0:T(8,128)(2,1)S(1)}, bf16[2048,128]{1,0:T(8,128)(2,1)S(1)}, u32[]{:S(2)}, u32[]{:S(2)}) collective-permute-start(bf16[2048,128]{1,0:T(8,128)(2,1)S(1)} %collective-permute-done.7.refs_10_), channel_id=1, source_target_pairs={{0,1},{1,0},{2,3},{3,2},{4,5},{5,4},{6,7},{7,6},{8,9},{9,8},{10,11... | collective-permute-start | bytes 1572872 | tf_op jit(solution)/shard_map/ppermute | solution.py:158
  25.1 14.3 %collective-permute-start.2 = (bf16[32,4096]{1,0:T(8,128)(2,1)S(1)}, bf16[32,4096]{1,0:T(8,128)(2,1)S(1)}, u32[]{:S(2)}, u32[]{:S(2)}) collective-permute-start(bf16[32,4096]{1,0:T(8,128)(2,1)S(1)} %get-tuple-element.16), channel_id=1, source_target_pairs={{0,12},{2,14},{4,8},{6,10},{8,4},{10,6},{12,0},{14,2},{1,13},{3,15... | collective-permute-start | bytes 786440 | tf_op jit(solution)/shard_map/ppermute | solution.py:154
  39.5 5.2 %copy-start.3 = (bf16[128,2048]{1,0:T(8,128)(2,1)S(1)}, bf16[128,2048]{1,0:T(8,128)(2,1)}, u32[]{:S(2)}) copy-start(bf16[128,2048]{1,0:T(8,128)(2,1)} %param.7) | copy-start | bytes 1572868
  40.2 6.4 %collective-permute-start.10 = (bf16[32,512]{1,0:T(8,128)(2,1)S(1)}, bf16[32,512]{1,0:T(8,128)(2,1)S(1)}, u32[]{:S(2)}, u32[]{:S(2)}) collective-permute-start(bf16[32,512]{1,0:T(8,128)(2,1)S(1)} %get-tuple-element.19), channel_id=1, source_target_pairs={{0,8},{2,10},{4,12},{6,14},{8,0},{10,2},{12,4},{14,6},{1,9},{3,11}... | collective-permute-start | bytes 98312 | tf_op jit(solution)/shard_map/ppermute | solution.py:154
  40.3 6.3 %collective-permute-start.11 = (bf16[32,512]{1,0:T(8,128)(2,1)S(1)}, bf16[32,512]{1,0:T(8,128)(2,1)S(1)}, u32[]{:S(2)}, u32[]{:S(2)}) collective-permute-start(bf16[32,512]{1,0:T(8,128)(2,1)S(1)} %get-tuple-element.20), channel_id=1, source_target_pairs={{0,12},{2,14},{4,8},{6,10},{8,4},{10,6},{12,0},{14,2},{1,13},{3,15... | collective-permute-start | bytes 98312 | tf_op jit(solution)/shard_map/ppermute | solution.py:154
  40.8 6.1 %collective-permute-start.9 = (bf16[32,512]{1,0:T(8,128)(2,1)S(1)}, bf16[32,512]{1,0:T(8,128)(2,1)S(1)}, u32[]{:S(2)}, u32[]{:S(2)}) collective-permute-start(bf16[32,512]{1,0:T(8,128)(2,1)S(1)} %get-tuple-element.18), channel_id=1, source_target_pairs={{0,4},{2,6},{4,0},{6,2},{8,12},{10,14},{12,8},{14,10},{1,5},{3,7},... | collective-permute-start | bytes 98312 | tf_op jit(solution)/shard_map/ppermute | solution.py:154
  44.7 14.0 %collective-permute-start.16 = (bf16[128,2048]{1,0:T(8,128)(2,1)S(1)}, bf16[128,2048]{1,0:T(8,128)(2,1)S(1)}, u32[]{:S(2)}, u32[]{:S(2)}) collective-permute-start(bf16[128,2048]{1,0:T(8,128)(2,1)S(1)} %copy-done.3), channel_id=1, source_target_pairs={{0,8},{2,10},{4,12},{6,14},{8,1},{10,3},{12,5},{14,7},{17,24},{19,... | collective-permute-start | bytes 1572872 | tf_op jit(solution)/shard_map/ppermute | solution.py:201
  47.0 13.6 %collective-permute-start.12 = (bf16[32,256]{1,0:T(8,128)(2,1)S(1)}, bf16[32,256]{1,0:T(8,128)(2,1)S(1)}, u32[]{:S(2)}, u32[]{:S(2)}) collective-permute-start(bf16[32,256]{1,0:T(8,128)(2,1)S(1)} %pad_maximum_fusion.1), channel_id=1, source_target_pairs={{0,1},{1,0},{2,3},{3,2},{4,5},{5,4},{6,7},{7,6},{8,9},{9,8},{10,11... | collective-permute-start | bytes 49160 | tf_op jit(solution)/shard_map/ppermute | solution.py:158
  47.1 14.2 %collective-permute-start.17 = (bf16[128,2048]{1,0:T(8,128)(2,1)S(1)}, bf16[128,2048]{1,0:T(8,128)(2,1)S(1)}, u32[]{:S(2)}, u32[]{:S(2)}) collective-permute-start(bf16[128,2048]{1,0:T(8,128)(2,1)S(1)} %copy-done.3), channel_id=1, source_target_pairs={{1,0},{3,2},{5,4},{7,6},{8,9},{10,11},{12,13},{14,15},{17,16},{19,... | collective-permute-start | bytes 1572872 | tf_op jit(solution)/shard_map/ppermute | solution.py:196
  58.6 11.1 %collective-permute-start.18 = (bf16[128,2048]{1,0:T(8,128)(2,1)S(1)}, bf16[128,2048]{1,0:T(8,128)(2,1)S(1)}, u32[]{:S(2)}, u32[]{:S(2)}) collective-permute-start(bf16[128,2048]{1,0:T(8,128)(2,1)S(1)} %collective-permute-done.16), channel_id=1, source_target_pairs={{1,17},{3,19},{5,21},{7,23},{8,24},{10,26},{12,28},{14,30},{17,1},... | collective-permute-start | bytes 1572872 | tf_op jit(solution)/shard_map/ppermute | solution.py:215
  60.6 13.0 %collective-permute-start.13 = (bf16[64,256]{1,0:T(8,128)(2,1)S(1)}, bf16[64,256]{1,0:T(8,128)(2,1)S(1)}, u32[]{:S(2)}, u32[]{:S(2)}) collective-permute-start(bf16[64,256]{1,0:T(8,128)(2,1)S(1)} %pad_maximum_fusion), channel_id=1, source_target_pairs={{0,2},{2,0},{4,6},{6,4},{8,10},{10,8},{12,14},{14,12},{1,3},{3,1},... | collective-permute-start | bytes 98312 | tf_op jit(solution)/shard_map/ppermute | solution.py:154
  69.8 5.7 %collective-permute-start.14 = (bf16[64,256]{1,0:T(8,128)(2,1)S(1)}, bf16[64,256]{1,0:T(8,128)(2,1)S(1)}, u32[]{:S(2)}, u32[]{:S(2)}) collective-permute-start(bf16[64,256]{1,0:T(8,128)(2,1)S(1)} %pad_maximum_fusion), channel_id=1, source_target_pairs={{0,4},{2,6},{4,0},{6,2},{8,12},{10,14},{12,8},{14,10},{1,5},{3,7},... | collective-permute-start | bytes 98312 | tf_op jit(solution)/shard_map/ppermute | solution.py:154
  73.6 4.8 %collective-permute-start.15 = (bf16[64,256]{1,0:T(8,128)(2,1)S(1)}, bf16[64,256]{1,0:T(8,128)(2,1)S(1)}, u32[]{:S(2)}, u32[]{:S(2)}) collective-permute-start(bf16[64,256]{1,0:T(8,128)(2,1)S(1)} %pad_maximum_fusion), channel_id=1, source_target_pairs={{0,6},{2,4},{4,2},{6,0},{8,14},{10,12},{12,10},{14,8},{1,7},{3,5},... | collective-permute-start | bytes 98312 | tf_op jit(solution)/shard_map/ppermute | solution.py:154
  79.0 6.4 %collective-permute-start.19 = (bf16[64,2048]{1,0:T(8,128)(2,1)S(1)}, bf16[64,2048]{1,0:T(8,128)(2,1)S(1)}, u32[]{:S(2)}, u32[]{:S(2)}) collective-permute-start(bf16[64,2048]{1,0:T(8,128)(2,1)S(1)} %get-tuple-element.29), channel_id=1, source_target_pairs={{0,2},{2,0},{4,6},{6,4},{8,10},{10,8},{12,14},{14,12},{1,3},{3,1},... | collective-permute-start | bytes 786440 | tf_op jit(solution)/shard_map/ppermute | solution.py:154
  79.5 6.4 %collective-permute-start.20 = (bf16[64,2048]{1,0:T(8,128)(2,1)S(1)}, bf16[64,2048]{1,0:T(8,128)(2,1)S(1)}, u32[]{:S(2)}, u32[]{:S(2)}) collective-permute-start(bf16[64,2048]{1,0:T(8,128)(2,1)S(1)} %get-tuple-element.28), channel_id=1, source_target_pairs={{0,4},{2,6},{4,0},{6,2},{8,12},{10,14},{12,8},{14,10},{1,5},{3,7},... | collective-permute-start | bytes 786440 | tf_op jit(solution)/shard_map/ppermute | solution.py:154
  80.0 9.7 %collective-permute-start.21 = (bf16[64,2048]{1,0:T(8,128)(2,1)S(1)}, bf16[64,2048]{1,0:T(8,128)(2,1)S(1)}, u32[]{:S(2)}, u32[]{:S(2)}) collective-permute-start(bf16[64,2048]{1,0:T(8,128)(2,1)S(1)} %get-tuple-element.27), channel_id=1, source_target_pairs={{0,6},{2,4},{4,2},{6,0},{8,14},{10,12},{12,10},{14,8},{1,7},{3,5},... | collective-permute-start | bytes 786440 | tf_op jit(solution)/shard_map/ppermute | solution.py:154

commit v2 on v1

--- a/solution.py
+++ b/solution.py
@@ -6,6 +6,8 @@
 from jax.experimental import pallas as pl
 from jax.experimental.pallas import tpu as pltpu
 from jax.sharding import PartitionSpec as P
+
+N_FAR = 2
 
 
 def in_order(parts, index):
@@ -120,6 +122,50 @@
     )(index.reshape(1), *blocks)
 
 
+def mixed_kernel(place, own_rows, beside_rows, *refs, n_hidden, n_far):
+    hidden, far = refs[:n_hidden], refs[n_hidden : n_hidden + 2 * n_far]
+    outs, down = refs[n_hidden + 2 * n_far : -1], refs[-1]
+    rows = hidden[0].shape[0]
+    units = own_rows.shape[0]
+    own, core, group = place[0], place[1], place[2]
+
+    @pl.when(own == 1)
+    def _():
+        down[pl.ds(pl.multiple_of(core * units, units), units)] = own_rows[...]
+        down[pl.ds(pl.multiple_of((1 - core) * units, units), units)] = beside_rows[...]
+
+    @pl.when(own != 1)
+    def _():
+        size = units // n_far
+        for k, piece in enumerate(far):
+            of = group if k < n_far else 1 - group
+            first = pl.multiple_of(of * units + k % n_far * size, size)
+            down[pl.ds(first, size)] = piece[...]
+
+    result = jnp.dot(
+        jnp.concatenate([h[...] for h in hidden], axis=0),
+        down[...],
+        preferred_element_type=jnp.float32,
+    )
+    for k, out in enumerate(outs):
+        out[...] = result[k * rows : (k + 1) * rows].astype(out.dtype)
+
+
+def mixed_blocks(place, own_rows, beside_rows, hidden, far):
+    rows = hidden[0].shape[0]
+    units, columns = own_rows.shape
+    vmem = pl.BlockSpec(memory_space=pltpu.VMEM)
+    return pl.pallas_call(
+        functools.partial(mixed_kernel, n_hidden=len(hidden), n_far=len(far) // 2),
+        out_shape=[jax.ShapeDtypeStruct((rows, columns), jnp.bfloat16)] * len(hidden),
+        in_specs=[pl.BlockSpec(memory_space=pltpu.SMEM)] + [vmem] * (2 + len(hidden) + len(far)),
+        out_specs=[vmem] * len(hidden),
+        scratch_shapes=[pltpu.VMEM((2 * units, columns), jnp.bfloat16)],
+        compiler_params=pltpu.CompilerParams(vmem_limit_bytes=16 * 1024 * 1024),
+        name="mixed_blocks",
+    )(place, own_rows, beside_rows, *hidden, *far)
+
+
 def per_device(tokens, gate_weight, up_weight, down_weight, *, n_groups, n_batch, n_mp):
     n_row = n_batch // n_mp
     rows = tokens.shape[0]
@@ -193,40 +239,28 @@
         hidden = jnp.concatenate(cores(hidden), axis=0)
 
         side = row // near
-        near_down = lax.ppermute(
-            down_weight,
-            axes,
-            [(device(r, a, 1 - r // near), device(r, a, r // near)) for r in range(n_row) for a in range(2)],
-        )
-        far_down = lax.ppermute(
-            down_weight,
-            ("groups", "batch", "mp"),
-            [
-                (
-                    g * n_batch * 2 + device(r, a, g),
-                    g * n_batch * 2 + device(r ^ near, a, r // near),
-                )
-                for g in range(2)
-                for r in range(n_row)
-                for a in range(2)
-            ],
-        )
+        near_down = others(down_weight, "mp", n_mp)[0]
+        wide = ("groups", "batch", "mp")
+        fetch = []
+        for g in range(2):
+            for r in range(n_row):
+                for a in range(2):
+                    at = g * n_batch * 2
+                    fetch.append((at + device(r, a, g), at + device(r ^ near, a, r // near)))
+                    fetch.append((at + device(r, a, 1 - g), at + device(r, a, r // near)))
         holders = [device(r, a, 1 - r // near) for r in range(n_row) for a in range(2)]
-        far_down_other = lax.ppermute(
-            far_down,
-            ("groups", "batch", "mp"),
-            [(g * n_batch * 2 + h, (1 - g) * n_batch * 2 + h) for g in range(2) for h in holders],
-        )
-        own = core == side
-        down = in_order(
-            [jnp.where(own, down_weight, far_down), jnp.where(own, near_down, far_down_other)],
-            jnp.where(own, core, group),
-        )
+        trade = [(g * n_batch * 2 + h, (1 - g) * n_batch * 2 + h) for g in range(2) for h in holders]
+        far = []
+        for part in range(N_FAR):
+            size_of = units // N_FAR
+            rows_of = down_weight[part * size_of : (part + 1) * size_of]
+            far.append(lax.ppermute(rows_of, wide, fetch))
+        for part in range(N_FAR):
+            far.append(lax.ppermute(far[part], wide, trade))
         peers = range(1, near * n_mp)
         gathered = [hidden] + [away(hidden, k) for k in peers]
-        result = dot(jnp.concatenate(gathered, axis=0), jnp.concatenate(down, axis=0))
-        result = result.astype(jnp.bfloat16)
-        blocks = [result[k * rows : (k + 1) * rows] for k in range(near * n_mp)]
+        flags = jnp.stack([(core == side).astype(jnp.int32), core, group])
+        blocks = list(mixed_blocks(flags, down_weight, near_down, gathered, far))
         for k in peers:
             blocks[k] = away(blocks[k], k)
         return place(batch % (near * n_mp), blocks)

time: 90.9 us -> 88.4 us (0.972)
  the two profiles are of different devices: /device:TPU:18 before, /device:TPU:0 now
where the time goes in v2:
time: 88.4 us; the launch traced here: 88.2 us
  waiting for transfers between devices  43.1 us (49%)
  starting transfers between devices  39.3 us (44%)
  Pallas kernels  3.74 us (4%)
  local copies, waits for them, and re-layouts  1.73 us (2%)
    ppermute x14, waiting for transfers between devices, away(): return lax.ppermute(value, 'batch', [(b, b ^ step) for b in range(n_batch)])  39.6 us
    ppermute x14, starting transfers between devices, away(): return lax.ppermute(value, 'batch', [(b, b ^ step) for b in range(n_batch)])  31 us
    ppermute x2, starting transfers between devices, halved_plan(): far.append(lax.ppermute(rows_of, wide, fetch))  6.28 us
    ppermute x2, waiting for transfers between devices, halved_plan(): far.append(lax.ppermute(rows_of, wide, fetch))  3.44 us
  transfers between devices with their start and end apart: 24, of which 10 were waited for; matrix products, arithmetic and copies ran while one was open for 0% of the time, Pallas kernels for 2%

profile of v2, /device:TPU:0, one launch (start us, length us, event | category | flops | bytes accessed | tf_op | source)
XLA Modules:
  0.0 88.2 jit_solution(6781305021675375141)
XLA Ops:
  0.0 0.0 copy-start
  0.0 3.0 %collective-permute-start.6 = (bf16[2048,128]{1,0:T(8,128)(2,1)}, bf16[2048,128]{1,0:T(8,128)(2,1)S(1)}, u32[]{:S(2)}, u32[]{:S(2)}) collective-permute-start(bf16[2048,128]{1,0:T(8,128)(2,1)} %refs_4_.1), channel_id=1, source_target_pairs={{0,2},{2,0},{4,6},{6,4},{8,10},{10,8},{12,14},{14,12},{1,3},{3,1},... | collective-permute-start | bytes 1572872 | tf_op jit(solution)/shard_map/ppermute | solution.py:200
  3.0 0.1 collective-permute-start.8
  3.0 0.1 stack.59.place
  3.1 0.0 copy-start.1
  3.1 1.6 %copy-done.1 = bf16[64,16384]{1,0:T(8,128)(2,1)S(1)} copy-done((bf16[64,16384]{1,0:T(8,128)(2,1)S(1)}, bf16[64,16384]{1,0:T(8,128)(2,1)}, u32[]{:S(2)}) %copy-start.1) | copy-done | bytes 2097176
  4.7 0.0 copy-start.2
  4.7 0.0 copy-start.3
  4.7 1.0 %cut.1 = (bf16[32,4096]{1,0:T(8,128)(2,1)S(1)}, bf16[32,4096]{1,0:T(8,128)(2,1)S(1)}, bf16[32,4096]{1,0:T(8,128)(2,1)S(1)}, bf16[32,4096]{1,0:T(8,128)(2,1)S(1)}) custom-call(s32[9]{0:T(128)S(1)} %stack.59.place, bf16[64,16384]{1,0:T(8,128)(2,1)S(1)} %copy-done.1), custom_call_target="tpu_custom_call" | custom-call | tf_op jit(solution)/shard_map/cut/pallas_call | solution.py:45
  5.7 2.1 %collective-permute-start.1 = (bf16[32,4096]{1,0:T(8,128)(2,1)S(1)}, bf16[32,4096]{1,0:T(8,128)(2,1)S(1)}, u32[]{:S(2)}, u32[]{:S(2)}) collective-permute-start(bf16[32,4096]{1,0:T(8,128)(2,1)S(1)} %get-tuple-element.18), channel_id=1, source_target_pairs={{0,4},{2,6},{4,0},{6,2},{8,12},{10,14},{12,8},{14,10},{1,5},{3,7},... | collective-permute-start | bytes 786440 | tf_op jit(solution)/shard_map/ppermute | solution.py:200
  7.8 2.6 %collective-permute-start.2 = (bf16[32,4096]{1,0:T(8,128)(2,1)S(1)}, bf16[32,4096]{1,0:T(8,128)(2,1)S(1)}, u32[]{:S(2)}, u32[]{:S(2)}) collective-permute-start(bf16[32,4096]{1,0:T(8,128)(2,1)S(1)} %get-tuple-element.19), channel_id=1, source_target_pairs={{0,8},{2,10},{4,12},{6,14},{8,0},{10,2},{12,4},{14,6},{1,9},{3,11}... | collective-permute-start | bytes 786440 | tf_op jit(solution)/shard_map/ppermute | solution.py:200
  10.4 0.0 copy-done.2
  10.4 0.0 collective-permute-start.4
  10.4 8.7 %collective-permute-done.1.refs_1_ = bf16[32,4096]{1,0:T(8,128)(2,1)S(1)} collective-permute-done((bf16[32,4096]{1,0:T(8,128)(2,1)S(1)}, bf16[32,4096]{1,0:T(8,128)(2,1)S(1)}, u32[]{:S(2)}, u32[]{:S(2)}) %collective-permute-start.1) | collective-permute-done | bytes 262176 | tf_op jit(solution)/shard_map/ppermute | solution.py:200
  19.1 0.0 copy-done.3
  19.1 0.0 collective-permute-start.5
  19.1 0.0 collective-permute-done.6.refs_8_
  19.1 0.5 collective-permute-start.7
  19.6 6.8 %collective-permute-done.8.refs_10_ = bf16[2048,128]{1,0:T(8,128)(2,1)S(1)} collective-permute-done((bf16[2048,128]{1,0:T(8,128)(2,1)}, bf16[2048,128]{1,0:T(8,128)(2,1)S(1)}, u32[]{:S(2)}, u32[]{:S(2)}) %collective-permute-start.8) | collective-permute-done | bytes 524320 | tf_op jit(solution)/shard_map/ppermute | solution.py:200
  26.3 0.0 collective-permute-start.9
  26.3 0.0 collective-permute-done.2.refs_2_
  26.3 3.9 %collective-permute-start.3 = (bf16[32,4096]{1,0:T(8,128)(2,1)S(1)}, bf16[32,4096]{1,0:T(8,128)(2,1)S(1)}, u32[]{:S(2)}, u32[]{:S(2)}) collective-permute-start(bf16[32,4096]{1,0:T(8,128)(2,1)S(1)} %get-tuple-element.20), channel_id=1, source_target_pairs={{0,12},{2,14},{4,8},{6,10},{8,4},{10,6},{12,0},{14,2},{1,13},{3,15... | collective-permute-start | bytes 786440 | tf_op jit(solution)/shard_map/ppermute | solution.py:200
  30.2 7.1 %collective-permute-done.3.refs_3_ = bf16[32,4096]{1,0:T(8,128)(2,1)S(1)} collective-permute-done((bf16[32,4096]{1,0:T(8,128)(2,1)S(1)}, bf16[32,4096]{1,0:T(8,128)(2,1)S(1)}, u32[]{:S(2)}, u32[]{:S(2)}) %collective-permute-start.3) | collective-permute-done | bytes 262176 | tf_op jit(solution)/shard_map/ppermute | solution.py:200
  37.3 0.0 copy-done
  37.3 0.0 collective-permute-start
  37.3 0.0 collective-permute-done.4.refs_5_
  37.3 0.0 collective-permute-done.5.refs_7_
  37.3 0.0 collective-permute-done.7.refs_9_
  37.3 0.0 collective-permute-done.9.refs_11_
  37.3 0.7 slab_sums.1
  38.0 5.3 %collective-permute-start.10 = (bf16[32,512]{1,0:T(8,128)(2,1)S(1)}, bf16[32,512]{1,0:T(8,128)(2,1)S(1)}, u32[]{:S(2)}, u32[]{:S(2)}) collective-permute-start(bf16[32,512]{1,0:T(8,128)(2,1)S(1)} %get-tuple-element.22), channel_id=1, source_target_pairs={{0,4},{2,6},{4,0},{6,2},{8,12},{10,14},{12,8},{14,10},{1,5},{3,7},... | collective-permute-start | bytes 98312 | tf_op jit(solution)/shard_map/ppermute | solution.py:200
  43.3 1.1 %collective-permute-start.11 = (bf16[32,512]{1,0:T(8,128)(2,1)S(1)}, bf16[32,512]{1,0:T(8,128)(2,1)S(1)}, u32[]{:S(2)}, u32[]{:S(2)}) collective-permute-start(bf16[32,512]{1,0:T(8,128)(2,1)S(1)} %get-tuple-element.23), channel_id=1, source_target_pairs={{0,8},{2,10},{4,12},{6,14},{8,0},{10,2},{12,4},{14,6},{1,9},{3,11}... | collective-permute-start | bytes 98312 | tf_op jit(solution)/shard_map/ppermute | solution.py:200
  44.4 1.4 %collective-permute-start.12 = (bf16[32,512]{1,0:T(8,128)(2,1)S(1)}, bf16[32,512]{1,0:T(8,128)(2,1)S(1)}, u32[]{:S(2)}, u32[]{:S(2)}) collective-permute-start(bf16[32,512]{1,0:T(8,128)(2,1)S(1)} %get-tuple-element.24), channel_id=1, source_target_pairs={{0,12},{2,14},{4,8},{6,10},{8,4},{10,6},{12,0},{14,2},{1,13},{3,15... | collective-permute-start | bytes 98312 | tf_op jit(solution)/shard_map/ppermute | solution.py:200
  45.9 3.9 %collective-permute-start.17 = (bf16[64,2048]{1,0:T(8,128)(2,1)S(1)}, bf16[64,2048]{1,0:T(8,128)(2,1)S(1)}, u32[]{:S(2)}, u32[]{:S(2)}) collective-permute-start(bf16[64,2048]{1,0:T(8,128)(2,1)S(1)} %get-tuple-element.30), channel_id=1, source_target_pairs={{0,8},{1,0},{2,10},{3,2},{4,12},{5,4},{6,14},{7,6},{8,1},{9,9},{10... | collective-permute-start | bytes 786440 | tf_op jit(solution)/shard_map/ppermute | solution.py:257
  49.8 0.0 collective-permute-done.10
  49.8 2.3 %collective-permute-start.18 = (bf16[64,2048]{1,0:T(8,128)(2,1)S(1)}, bf16[64,2048]{1,0:T(8,128)(2,1)S(1)}, u32[]{:S(2)}, u32[]{:S(2)}) collective-permute-start(bf16[64,2048]{1,0:T(8,128)(2,1)S(1)} %get-tuple-element.29), channel_id=1, source_target_pairs={{0,8},{1,0},{2,10},{3,2},{4,12},{5,4},{6,14},{7,6},{8,1},{9,9},{10... | collective-permute-start | bytes 786440 | tf_op jit(solution)/shard_map/ppermute | solution.py:257
  52.2 0.0 collective-permute-done.11
  52.2 0.0 collective-permute-done.12
  52.3 0.1 collective-permute-start.13
  52.4 1.3 %collective-permute-done.17.refs_4_ = bf16[64,2048]{1,0:T(8,128)(2,1)S(1)} collective-permute-done((bf16[64,2048]{1,0:T(8,128)(2,1)S(1)}, bf16[64,2048]{1,0:T(8,128)(2,1)S(1)}, u32[]{:S(2)}, u32[]{:S(2)}) %collective-permute-start.17) | collective-permute-done | bytes 262176 | tf_op jit(solution)/shard_map/ppermute | solution.py:257
  53.7 0.7 collective-permute-start.19
  54.4 2.1 %collective-permute-done.18.refs_5_ = bf16[64,2048]{1,0:T(8,128)(2,1)S(1)} collective-permute-done((bf16[64,2048]{1,0:T(8,128)(2,1)S(1)}, bf16[64,2048]{1,0:T(8,128)(2,1)S(1)}, u32[]{:S(2)}, u32[]{:S(2)}) %collective-permute-start.18) | collective-permute-done | bytes 262176 | tf_op jit(solution)/shard_map/ppermute | solution.py:257
  56.5 0.7 collective-permute-start.20
  57.2 0.0 collective-permute-done.13
  57.2 1.6 %collective-permute-start.14 = (bf16[64,256]{1,0:T(8,128)(2,1)S(1)}, bf16[64,256]{1,0:T(8,128)(2,1)S(1)}, u32[]{:S(2)}, u32[]{:S(2)}) collective-permute-start(bf16[64,256]{1,0:T(8,128)(2,1)S(1)} %pad_maximum_fusion.refs_0_), channel_id=1, source_target_pairs={{0,2},{2,0},{4,6},{6,4},{8,10},{10,8},{12,14},{14,12},{1,3},{3,1},... | collective-permute-start | bytes 98312 | tf_op jit(solution)/shard_map/ppermute | solution.py:200
  58.8 6.5 %collective-permute-start.15 = (bf16[64,256]{1,0:T(8,128)(2,1)S(1)}, bf16[64,256]{1,0:T(8,128)(2,1)S(1)}, u32[]{:S(2)}, u32[]{:S(2)}) collective-permute-start(bf16[64,256]{1,0:T(8,128)(2,1)S(1)} %pad_maximum_fusion.refs_0_), channel_id=1, source_target_pairs={{0,4},{2,6},{4,0},{6,2},{8,12},{10,14},{12,8},{14,10},{1,5},{3,7},... | collective-permute-start | bytes 98312 | tf_op jit(solution)/shard_map/ppermute | solution.py:200
  65.4 0.0 collective-permute-done.19.refs_6_
  65.4 0.0 collective-permute-start.16
  65.4 0.1 pad_add_fusion.place
  65.4 0.0 collective-permute-done.20.refs_7_
  65.4 0.0 collective-permute-done.beside_rows
  65.4 0.0 collective-permute-done.14.refs_1_
  65.5 1.8 %collective-permute-done.15.refs_2_ = bf16[64,256]{1,0:T(8,128)(2,1)S(1)} collective-permute-done((bf16[64,256]{1,0:T(8,128)(2,1)S(1)}, bf16[64,256]{1,0:T(8,128)(2,1)S(1)}, u32[]{:S(2)}, u32[]{:S(2)}) %collective-permute-start.15) | collective-permute-done | bytes 32800 | tf_op jit(solution)/shard_map/ppermute | solution.py:200
  67.2 3.1 %collective-permute-done.16.refs_3_ = bf16[64,256]{1,0:T(8,128)(2,1)S(1)} collective-permute-done((bf16[64,256]{1,0:T(8,128)(2,1)S(1)}, bf16[64,256]{1,0:T(8,128)(2,1)S(1)}, u32[]{:S(2)}, u32[]{:S(2)}) %collective-permute-start.16) | collective-permute-done | bytes 32800 | tf_op jit(solution)/shard_map/ppermute | solution.py:200
  70.3 1.1 %mixed_blocks.1 = (bf16[64,2048]{1,0:T(8,128)(2,1)S(1)}, bf16[64,2048]{1,0:T(8,128)(2,1)S(1)}, bf16[64,2048]{1,0:T(8,128)(2,1)S(1)}, bf16[64,2048]{1,0:T(8,128)(2,1)S(1)}) custom-call(s32[3]{0:T(128)S(1)} %pad_add_fusion.place, bf16[128,2048]{1,0:T(8,128)(2,1)S(1)} %copy-done, bf16[128,2048]{1,0:T(8,128)(2,1)S(1)} %collective-permute-done.beside_rows, ...), custom_call_target="tpu_custom_call" | custom-call | tf_op jit(solution)/shard_map/mixed_blocks/pallas_call | solution.py:158
  71.4 0.5 collective-permute-start.21
  71.8 0.4 collective-permute-start.22
  72.2 2.7 %collective-permute-start.23 = (bf16[64,2048]{1,0:T(8,128)(2,1)S(1)}, bf16[64,2048]{1,0:T(8,128)(2,1)S(1)}, u32[]{:S(2)}, u32[]{:S(2)}) collective-permute-start(bf16[64,2048]{1,0:T(8,128)(2,1)S(1)} %get-tuple-element.28), channel_id=1, source_target_pairs={{0,6},{2,4},{4,2},{6,0},{8,14},{10,12},{12,10},{14,8},{1,7},{3,5},... | collective-permute-start | bytes 786440 | tf_op jit(solution)/shard_map/ppermute | solution.py:200
  74.9 5.4 %collective-permute-done.21.refs_1_ = bf16[64,2048]{1,0:T(8,128)(2,1)S(1)} collective-permute-done((bf16[64,2048]{1,0:T(8,128)(2,1)S(1)}, bf16[64,2048]{1,0:T(8,128)(2,1)S(1)}, u32[]{:S(2)}, u32[]{:S(2)}) %collective-permute-start.21) | collective-permute-done | bytes 262176 | tf_op jit(solution)/shard_map/ppermute | solution.py:200
  80.4 0.3 collective-permute-done.22.refs_2_
  80.7 6.5 %collective-permute-done.23.refs_3_ = bf16[64,2048]{1,0:T(8,128)(2,1)S(1)} collective-permute-done((bf16[64,2048]{1,0:T(8,128)(2,1)S(1)}, bf16[64,2048]{1,0:T(8,128)(2,1)S(1)}, u32[]{:S(2)}, u32[]{:S(2)}) %collective-permute-start.23) | collective-permute-done | bytes 262176 | tf_op jit(solution)/shard_map/ppermute | solution.py:200
  87.2 1.0 %place.1 = bf16[64,8192]{1,0:T(8,128)(2,1)} custom-call(s32[1]{0:T(128)} %bitcast.index, bf16[64,2048]{1,0:T(8,128)(2,1)S(1)} %get-tuple-element.25.refs_0_, bf16[64,2048]{1,0:T(8,128)(2,1)S(1)} %collective-permute-done.21.refs_1_, bf16[64,2048]{1,0:T(8,128)(2,1)S(1)} %collective-permute-done.22.refs_2_, bf16[64,2048]{1,0:T(8,128)(2,1)S(1)} %collective-permute-done.23.refs_3_), custom_call_target="tpu_custom_call" | custom-call | tf_op jit(solution)/shard_map/place/pallas_call | solution.py:114
  (7 shorter events, 0.1 us)
Async XLA Ops:
  0.0 37.3 %copy-start = (bf16[128,2048]{1,0:T(8,128)(2,1)S(1)}, bf16[128,2048]{1,0:T(8,128)(2,1)}, u32[]{:S(2)}) copy-start(bf16[128,2048]{1,0:T(8,128)(2,1)} %own_rows.1) | copy-start | bytes 1572868
  0.0 19.1 %collective-permute-start.6 = (bf16[2048,128]{1,0:T(8,128)(2,1)}, bf16[2048,128]{1,0:T(8,128)(2,1)S(1)}, u32[]{:S(2)}, u32[]{:S(2)}) collective-permute-start(bf16[2048,128]{1,0:T(8,128)(2,1)} %refs_4_.1), channel_id=1, source_target_pairs={{0,2},{2,0},{4,6},{6,4},{8,10},{10,8},{12,14},{14,12},{1,3},{3,1},... | collective-permute-start | bytes 1572872 | tf_op jit(solution)/shard_map/ppermute | solution.py:200
  3.0 23.4 %collective-permute-start.8 = (bf16[2048,128]{1,0:T(8,128)(2,1)}, bf16[2048,128]{1,0:T(8,128)(2,1)S(1)}, u32[]{:S(2)}, u32[]{:S(2)}) collective-permute-start(bf16[2048,128]{1,0:T(8,128)(2,1)} %refs_6_.1), channel_id=1, source_target_pairs={{0,2},{2,0},{4,6},{6,4},{8,10},{10,8},{12,14},{14,12},{1,3},{3,1},... | collective-permute-start | bytes 1572872 | tf_op jit(solution)/shard_map/ppermute | solution.py:200
  3.1 1.6 %copy-start.1 = (bf16[64,16384]{1,0:T(8,128)(2,1)S(1)}, bf16[64,16384]{1,0:T(8,128)(2,1)}, u32[]{:S(2)}) copy-start(bf16[64,16384]{1,0:T(8,128)(2,1)} %tokens.1) | copy-start | bytes 6291460
  4.7 5.7 %copy-start.2 = (bf16[2048,128]{1,0:T(8,128)(2,1)S(1)}, bf16[2048,128]{1,0:T(8,128)(2,1)}, u32[]{:S(2)}) copy-start(bf16[2048,128]{1,0:T(8,128)(2,1)} %refs_4_.1) | copy-start | bytes 1572868
  4.7 14.3 %copy-start.3 = (bf16[2048,128]{1,0:T(8,128)(2,1)S(1)}, bf16[2048,128]{1,0:T(8,128)(2,1)}, u32[]{:S(2)}) copy-start(bf16[2048,128]{1,0:T(8,128)(2,1)} %refs_6_.1) | copy-start | bytes 1572868
  5.7 13.4 %collective-permute-start.1 = (bf16[32,4096]{1,0:T(8,128)(2,1)S(1)}, bf16[32,4096]{1,0:T(8,128)(2,1)S(1)}, u32[]{:S(2)}, u32[]{:S(2)}) collective-permute-start(bf16[32,4096]{1,0:T(8,128)(2,1)S(1)} %get-tuple-element.18), channel_id=1, source_target_pairs={{0,4},{2,6},{4,0},{6,2},{8,12},{10,14},{12,8},{14,10},{1,5},{3,7},... | collective-permute-start | bytes 786440 | tf_op jit(solution)/shard_map/ppermute | solution.py:200
  7.8 18.5 %collective-permute-start.2 = (bf16[32,4096]{1,0:T(8,128)(2,1)S(1)}, bf16[32,4096]{1,0:T(8,128)(2,1)S(1)}, u32[]{:S(2)}, u32[]{:S(2)}) collective-permute-start(bf16[32,4096]{1,0:T(8,128)(2,1)S(1)} %get-tuple-element.19), channel_id=1, source_target_pairs={{0,8},{2,10},{4,12},{6,14},{8,0},{10,2},{12,4},{14,6},{1,9},{3,11}... | collective-permute-start | bytes 786440 | tf_op jit(solution)/shard_map/ppermute | solution.py:200
  10.4 26.9 %collective-permute-start.4 = (bf16[2048,128]{1,0:T(8,128)(2,1)S(1)}, bf16[2048,128]{1,0:T(8,128)(2,1)S(1)}, u32[]{:S(2)}, u32[]{:S(2)}) collective-permute-start(bf16[2048,128]{1,0:T(8,128)(2,1)S(1)} %copy-done.2), channel_id=1, source_target_pairs={{0,1},{1,0},{2,3},{3,2},{4,5},{5,4},{6,7},{7,6},{8,9},{9,8},{10,11... | collective-permute-start | bytes 1572872 | tf_op jit(solution)/shard_map/ppermute | solution.py:204
  19.1 18.2 %collective-permute-start.5 = (bf16[2048,128]{1,0:T(8,128)(2,1)S(1)}, bf16[2048,128]{1,0:T(8,128)(2,1)S(1)}, u32[]{:S(2)}, u32[]{:S(2)}) collective-permute-start(bf16[2048,128]{1,0:T(8,128)(2,1)S(1)} %copy-done.3), channel_id=1, source_target_pairs={{0,1},{1,0},{2,3},{3,2},{4,5},{5,4},{6,7},{7,6},{8,9},{9,8},{10,11... | collective-permute-start | bytes 1572872 | tf_op jit(solution)/shard_map/ppermute | solution.py:204
  19.1 18.2 %collective-permute-start.7 = (bf16[2048,128]{1,0:T(8,128)(2,1)S(1)}, bf16[2048,128]{1,0:T(8,128)(2,1)S(1)}, u32[]{:S(2)}, u32[]{:S(2)}) collective-permute-start(bf16[2048,128]{1,0:T(8,128)(2,1)S(1)} %collective-permute-done.6.refs_8_), channel_id=1, source_target_pairs={{0,1},{1,0},{2,3},{3,2},{4,5},{5,4},{6,7},{7,6},{8,9},{9,8},{10,11... | collective-permute-start | bytes 1572872 | tf_op jit(solution)/shard_map/ppermute | solution.py:204
  26.3 11.0 %collective-permute-start.9 = (bf16[2048,128]{1,0:T(8,128)(2,1)S(1)}, bf16[2048,128]{1,0:T(8,128)(2,1)S(1)}, u32[]{:S(2)}, u32[]{:S(2)}) collective-permute-start(bf16[2048,128]{1,0:T(8,128)(2,1)S(1)} %collective-permute-done.8.refs_10_), channel_id=1, source_target_pairs={{0,1},{1,0},{2,3},{3,2},{4,5},{5,4},{6,7},{7,6},{8,9},{9,8},{10,11... | collective-permute-start | bytes 1572872 | tf_op jit(solution)/shard_map/ppermute | solution.py:204
  26.3 10.9 %collective-permute-start.3 = (bf16[32,4096]{1,0:T(8,128)(2,1)S(1)}, bf16[32,4096]{1,0:T(8,128)(2,1)S(1)}, u32[]{:S(2)}, u32[]{:S(2)}) collective-permute-start(bf16[32,4096]{1,0:T(8,128)(2,1)S(1)} %get-tuple-element.20), channel_id=1, source_target_pairs={{0,12},{2,14},{4,8},{6,10},{8,4},{10,6},{12,0},{14,2},{1,13},{3,15... | collective-permute-start | bytes 786440 | tf_op jit(solution)/shard_map/ppermute | solution.py:200
  37.3 28.2 %collective-permute-start = (bf16[128,2048]{1,0:T(8,128)(2,1)S(1)}, bf16[128,2048]{1,0:T(8,128)(2,1)S(1)}, u32[]{:S(2)}, u32[]{:S(2)}) collective-permute-start(bf16[128,2048]{1,0:T(8,128)(2,1)S(1)} %copy-done), channel_id=1, source_target_pairs={{0,1},{1,0},{2,3},{3,2},{4,5},{5,4},{6,7},{7,6},{8,9},{9,8},{10,11... | collective-permute-start | bytes 1572872 | tf_op jit(solution)/shard_map/ppermute | solution.py:204
  38.0 11.8 %collective-permute-start.10 = (bf16[32,512]{1,0:T(8,128)(2,1)S(1)}, bf16[32,512]{1,0:T(8,128)(2,1)S(1)}, u32[]{:S(2)}, u32[]{:S(2)}) collective-permute-start(bf16[32,512]{1,0:T(8,128)(2,1)S(1)} %get-tuple-element.22), channel_id=1, source_target_pairs={{0,4},{2,6},{4,0},{6,2},{8,12},{10,14},{12,8},{14,10},{1,5},{3,7},... | collective-permute-start | bytes 98312 | tf_op jit(solution)/shard_map/ppermute | solution.py:200
  43.3 8.8 %collective-permute-start.11 = (bf16[32,512]{1,0:T(8,128)(2,1)S(1)}, bf16[32,512]{1,0:T(8,128)(2,1)S(1)}, u32[]{:S(2)}, u32[]{:S(2)}) collective-permute-start(bf16[32,512]{1,0:T(8,128)(2,1)S(1)} %get-tuple-element.23), channel_id=1, source_target_pairs={{0,8},{2,10},{4,12},{6,14},{8,0},{10,2},{12,4},{14,6},{1,9},{3,11}... | collective-permute-start | bytes 98312 | tf_op jit(solution)/shard_map/ppermute | solution.py:200
  44.4 7.8 %collective-permute-start.12 = (bf16[32,512]{1,0:T(8,128)(2,1)S(1)}, bf16[32,512]{1,0:T(8,128)(2,1)S(1)}, u32[]{:S(2)}, u32[]{:S(2)}) collective-permute-start(bf16[32,512]{1,0:T(8,128)(2,1)S(1)} %get-tuple-element.24), channel_id=1, source_target_pairs={{0,12},{2,14},{4,8},{6,10},{8,4},{10,6},{12,0},{14,2},{1,13},{3,15... | collective-permute-start | bytes 98312 | tf_op jit(solution)/shard_map/ppermute | solution.py:200
  45.9 7.9 %collective-permute-start.17 = (bf16[64,2048]{1,0:T(8,128)(2,1)S(1)}, bf16[64,2048]{1,0:T(8,128)(2,1)S(1)}, u32[]{:S(2)}, u32[]{:S(2)}) collective-permute-start(bf16[64,2048]{1,0:T(8,128)(2,1)S(1)} %get-tuple-element.30), channel_id=1, source_target_pairs={{0,8},{1,0},{2,10},{3,2},{4,12},{5,4},{6,14},{7,6},{8,1},{9,9},{10... | collective-permute-start | bytes 786440 | tf_op jit(solution)/shard_map/ppermute | solution.py:257
  49.8 6.7 %collective-permute-start.18 = (bf16[64,2048]{1,0:T(8,128)(2,1)S(1)}, bf16[64,2048]{1,0:T(8,128)(2,1)S(1)}, u32[]{:S(2)}, u32[]{:S(2)}) collective-permute-start(bf16[64,2048]{1,0:T(8,128)(2,1)S(1)} %get-tuple-element.29), channel_id=1, source_target_pairs={{0,8},{1,0},{2,10},{3,2},{4,12},{5,4},{6,14},{7,6},{8,1},{9,9},{10... | collective-permute-start | bytes 786440 | tf_op jit(solution)/shard_map/ppermute | solution.py:257
  52.3 4.9 %collective-permute-start.13 = (bf16[32,256]{1,0:T(8,128)(2,1)S(1)}, bf16[32,256]{1,0:T(8,128)(2,1)S(1)}, u32[]{:S(2)}, u32[]{:S(2)}) collective-permute-start(bf16[32,256]{1,0:T(8,128)(2,1)S(1)} %pad_maximum_fusion.1), channel_id=1, source_target_pairs={{0,1},{1,0},{2,3},{3,2},{4,5},{5,4},{6,7},{7,6},{8,9},{9,8},{10,11... | collective-permute-start | bytes 49160 | tf_op jit(solution)/shard_map/ppermute | solution.py:204
  53.7 11.6 %collective-permute-start.19 = (bf16[64,2048]{1,0:T(8,128)(2,1)S(1)}, bf16[64,2048]{1,0:T(8,128)(2,1)S(1)}, u32[]{:S(2)}, u32[]{:S(2)}) collective-permute-start(bf16[64,2048]{1,0:T(8,128)(2,1)S(1)} %collective-permute-done.17.refs_4_), channel_id=1, source_target_pairs={{1,17},{3,19},{5,21},{7,23},{8,24},{10,26},{12,28},{14,30},{17,1},... | collective-permute-start | bytes 786440 | tf_op jit(solution)/shard_map/ppermute | solution.py:259
  56.5 8.9 %collective-permute-start.20 = (bf16[64,2048]{1,0:T(8,128)(2,1)S(1)}, bf16[64,2048]{1,0:T(8,128)(2,1)S(1)}, u32[]{:S(2)}, u32[]{:S(2)}) collective-permute-start(bf16[64,2048]{1,0:T(8,128)(2,1)S(1)} %collective-permute-done.18.refs_5_), channel_id=1, source_target_pairs={{1,17},{3,19},{5,21},{7,23},{8,24},{10,26},{12,28},{14,30},{17,1},... | collective-permute-start | bytes 786440 | tf_op jit(solution)/shard_map/ppermute | solution.py:259
  57.2 8.2 %collective-permute-start.14 = (bf16[64,256]{1,0:T(8,128)(2,1)S(1)}, bf16[64,256]{1,0:T(8,128)(2,1)S(1)}, u32[]{:S(2)}, u32[]{:S(2)}) collective-permute-start(bf16[64,256]{1,0:T(8,128)(2,1)S(1)} %pad_maximum_fusion.refs_0_), channel_id=1, source_target_pairs={{0,2},{2,0},{4,6},{6,4},{8,10},{10,8},{12,14},{14,12},{1,3},{3,1},... | collective-permute-start | bytes 98312 | tf_op jit(solution)/shard_map/ppermute | solution.py:200
  58.8 8.4 %collective-permute-start.15 = (bf16[64,256]{1,0:T(8,128)(2,1)S(1)}, bf16[64,256]{1,0:T(8,128)(2,1)S(1)}, u32[]{:S(2)}, u32[]{:S(2)}) collective-permute-start(bf16[64,256]{1,0:T(8,128)(2,1)S(1)} %pad_maximum_fusion.refs_0_), channel_id=1, source_target_pairs={{0,4},{2,6},{4,0},{6,2},{8,12},{10,14},{12,8},{14,10},{1,5},{3,7},... | collective-permute-start | bytes 98312 | tf_op jit(solution)/shard_map/ppermute | solution.py:200
  65.4 5.0 %collective-permute-start.16 = (bf16[64,256]{1,0:T(8,128)(2,1)S(1)}, bf16[64,256]{1,0:T(8,128)(2,1)S(1)}, u32[]{:S(2)}, u32[]{:S(2)}) collective-permute-start(bf16[64,256]{1,0:T(8,128)(2,1)S(1)} %pad_maximum_fusion.refs_0_), channel_id=1, source_target_pairs={{0,6},{2,4},{4,2},{6,0},{8,14},{10,12},{12,10},{14,8},{1,7},{3,5},... | collective-permute-start | bytes 98312 | tf_op jit(solution)/shard_map/ppermute | solution.py:200
  71.4 9.0 %collective-permute-start.21 = (bf16[64,2048]{1,0:T(8,128)(2,1)S(1)}, bf16[64,2048]{1,0:T(8,128)(2,1)S(1)}, u32[]{:S(2)}, u32[]{:S(2)}) collective-permute-start(bf16[64,2048]{1,0:T(8,128)(2,1)S(1)} %get-tuple-element.26), channel_id=1, source_target_pairs={{0,2},{2,0},{4,6},{6,4},{8,10},{10,8},{12,14},{14,12},{1,3},{3,1},... | collective-permute-start | bytes 786440 | tf_op jit(solution)/shard_map/ppermute | solution.py:200
  71.8 8.9 %collective-permute-start.22 = (bf16[64,2048]{1,0:T(8,128)(2,1)S(1)}, bf16[64,2048]{1,0:T(8,128)(2,1)S(1)}, u32[]{:S(2)}, u32[]{:S(2)}) collective-permute-start(bf16[64,2048]{1,0:T(8,128)(2,1)S(1)} %get-tuple-element.27), channel_id=1, source_target_pairs={{0,4},{2,6},{4,0},{6,2},{8,12},{10,14},{12,8},{14,10},{1,5},{3,7},... | collective-permute-start | bytes 786440 | tf_op jit(solution)/shard_map/ppermute | solution.py:200
  72.2 15.0 %collective-permute-start.23 = (bf16[64,2048]{1,0:T(8,128)(2,1)S(1)}, bf16[64,2048]{1,0:T(8,128)(2,1)S(1)}, u32[]{:S(2)}, u32[]{:S(2)}) collective-permute-start(bf16[64,2048]{1,0:T(8,128)(2,1)S(1)} %get-tuple-element.28), channel_id=1, source_target_pairs={{0,6},{2,4},{4,2},{6,0},{8,14},{10,12},{12,10},{14,8},{1,7},{3,5},... | collective-permute-start | bytes 786440 | tf_op jit(solution)/shard_map/ppermute | solution.py:200

commit v3 on v2

--- a/solution.py
+++ b/solution.py
@@ -249,7 +249,11 @@
                     fetch.append((at + device(r, a, g), at + device(r ^ near, a, r // near)))
                     fetch.append((at + device(r, a, 1 - g), at + device(r, a, r // near)))
         holders = [device(r, a, 1 - r // near) for r in range(n_row) for a in range(2)]
-        trade = [(g * n_batch * 2 + h, (1 - g) * n_batch * 2 + h) for g in range(2) for h in holders]
+        trade = [
+            (g * n_batch * 2 + h, ((1 - g) if h in holders else g) * n_batch * 2 + h)
+            for g in range(2)
+            for h in range(n_batch * 2)
+        ]
         far = []
         for part in range(N_FAR):
             size_of = units // N_FAR

time: 88.4 us -> 88.4 us (level)
  no operation moved by 1% of the time
where the time goes in v3:
time: 88.4 us; the launch traced here: 88.2 us
  waiting for transfers between devices  43.1 us (49%)
  starting transfers between devices  39.3 us (44%)
  Pallas kernels  3.74 us (4%)
  local copies, waits for them, and re-layouts  1.73 us (2%)
    ppermute x14, waiting for transfers between devices, away(): return lax.ppermute(value, 'batch', [(b, b ^ step) for b in range(n_batch)])  39.6 us
    ppermute x14, starting transfers between devices, away(): return lax.ppermute(value, 'batch', [(b, b ^ step) for b in range(n_batch)])  31 us
    ppermute x2, starting transfers between devices, halved_plan(): far.append(lax.ppermute(rows_of, wide, fetch))  6.28 us
    ppermute x2, waiting for transfers between devices, halved_plan(): far.append(lax.ppermute(rows_of, wide, fetch))  3.44 us
  transfers between devices with their start and end apart: 24, of which 10 were waited for; matrix products, arithmetic and copies ran while one was open for 0% of the time, Pallas kernels for 2%

profile of v3, /device:TPU:0, one launch (start us, length us, event | category | flops | bytes accessed | tf_op | source)
XLA Modules:
  0.0 88.2 jit_solution(16380342555563765975)
XLA Ops:
  0.0 0.0 copy-start
  0.0 3.0 %collective-permute-start.6 = (bf16[2048,128]{1,0:T(8,128)(2,1)}, bf16[2048,128]{1,0:T(8,128)(2,1)S(1)}, u32[]{:S(2)}, u32[]{:S(2)}) collective-permute-start(bf16[2048,128]{1,0:T(8,128)(2,1)} %refs_4_.1), channel_id=1, source_target_pairs={{0,2},{2,0},{4,6},{6,4},{8,10},{10,8},{12,14},{14,12},{1,3},{3,1},... | collective-permute-start | bytes 1572872 | tf_op jit(solution)/shard_map/ppermute | solution.py:200
  3.0 0.1 collective-permute-start.8
  3.0 0.1 stack.59.place
  3.1 0.0 copy-start.1
  3.1 1.6 %copy-done.1 = bf16[64,16384]{1,0:T(8,128)(2,1)S(1)} copy-done((bf16[64,16384]{1,0:T(8,128)(2,1)S(1)}, bf16[64,16384]{1,0:T(8,128)(2,1)}, u32[]{:S(2)}) %copy-start.1) | copy-done | bytes 2097176
  4.7 0.0 copy-start.2
  4.7 0.0 copy-start.3
  4.7 1.0 %cut.1 = (bf16[32,4096]{1,0:T(8,128)(2,1)S(1)}, bf16[32,4096]{1,0:T(8,128)(2,1)S(1)}, bf16[32,4096]{1,0:T(8,128)(2,1)S(1)}, bf16[32,4096]{1,0:T(8,128)(2,1)S(1)}) custom-call(s32[9]{0:T(128)S(1)} %stack.59.place, bf16[64,16384]{1,0:T(8,128)(2,1)S(1)} %copy-done.1), custom_call_target="tpu_custom_call" | custom-call | tf_op jit(solution)/shard_map/cut/pallas_call | solution.py:45
  5.7 2.1 %collective-permute-start.1 = (bf16[32,4096]{1,0:T(8,128)(2,1)S(1)}, bf16[32,4096]{1,0:T(8,128)(2,1)S(1)}, u32[]{:S(2)}, u32[]{:S(2)}) collective-permute-start(bf16[32,4096]{1,0:T(8,128)(2,1)S(1)} %get-tuple-element.18), channel_id=1, source_target_pairs={{0,4},{2,6},{4,0},{6,2},{8,12},{10,14},{12,8},{14,10},{1,5},{3,7},... | collective-permute-start | bytes 786440 | tf_op jit(solution)/shard_map/ppermute | solution.py:200
  7.8 2.6 %collective-permute-start.2 = (bf16[32,4096]{1,0:T(8,128)(2,1)S(1)}, bf16[32,4096]{1,0:T(8,128)(2,1)S(1)}, u32[]{:S(2)}, u32[]{:S(2)}) collective-permute-start(bf16[32,4096]{1,0:T(8,128)(2,1)S(1)} %get-tuple-element.19), channel_id=1, source_target_pairs={{0,8},{2,10},{4,12},{6,14},{8,0},{10,2},{12,4},{14,6},{1,9},{3,11}... | collective-permute-start | bytes 786440 | tf_op jit(solution)/shard_map/ppermute | solution.py:200
  10.4 0.0 copy-done.2
  10.4 0.0 collective-permute-start.4
  10.4 8.7 %collective-permute-done.1.refs_1_ = bf16[32,4096]{1,0:T(8,128)(2,1)S(1)} collective-permute-done((bf16[32,4096]{1,0:T(8,128)(2,1)S(1)}, bf16[32,4096]{1,0:T(8,128)(2,1)S(1)}, u32[]{:S(2)}, u32[]{:S(2)}) %collective-permute-start.1) | collective-permute-done | bytes 262176 | tf_op jit(solution)/shard_map/ppermute | solution.py:200
  19.1 0.0 copy-done.3
  19.1 0.0 collective-permute-start.5
  19.1 0.0 collective-permute-done.6.refs_8_
  19.1 0.5 collective-permute-start.7
  19.6 6.8 %collective-permute-done.8.refs_10_ = bf16[2048,128]{1,0:T(8,128)(2,1)S(1)} collective-permute-done((bf16[2048,128]{1,0:T(8,128)(2,1)}, bf16[2048,128]{1,0:T(8,128)(2,1)S(1)}, u32[]{:S(2)}, u32[]{:S(2)}) %collective-permute-start.8) | collective-permute-done | bytes 524320 | tf_op jit(solution)/shard_map/ppermute | solution.py:200
  26.3 0.0 collective-permute-start.9
  26.3 0.0 collective-permute-done.2.refs_2_
  26.3 3.9 %collective-permute-start.3 = (bf16[32,4096]{1,0:T(8,128)(2,1)S(1)}, bf16[32,4096]{1,0:T(8,128)(2,1)S(1)}, u32[]{:S(2)}, u32[]{:S(2)}) collective-permute-start(bf16[32,4096]{1,0:T(8,128)(2,1)S(1)} %get-tuple-element.20), channel_id=1, source_target_pairs={{0,12},{2,14},{4,8},{6,10},{8,4},{10,6},{12,0},{14,2},{1,13},{3,15... | collective-permute-start | bytes 786440 | tf_op jit(solution)/shard_map/ppermute | solution.py:200
  30.2 7.1 %collective-permute-done.3.refs_3_ = bf16[32,4096]{1,0:T(8,128)(2,1)S(1)} collective-permute-done((bf16[32,4096]{1,0:T(8,128)(2,1)S(1)}, bf16[32,4096]{1,0:T(8,128)(2,1)S(1)}, u32[]{:S(2)}, u32[]{:S(2)}) %collective-permute-start.3) | collective-permute-done | bytes 262176 | tf_op jit(solution)/shard_map/ppermute | solution.py:200
  37.3 0.0 copy-done
  37.3 0.0 collective-permute-start
  37.3 0.0 collective-permute-done.4.refs_5_
  37.3 0.0 collective-permute-done.5.refs_7_
  37.3 0.0 collective-permute-done.7.refs_9_
  37.3 0.0 collective-permute-done.9.refs_11_
  37.3 0.7 slab_sums.1
  38.0 5.3 %collective-permute-start.10 = (bf16[32,512]{1,0:T(8,128)(2,1)S(1)}, bf16[32,512]{1,0:T(8,128)(2,1)S(1)}, u32[]{:S(2)}, u32[]{:S(2)}) collective-permute-start(bf16[32,512]{1,0:T(8,128)(2,1)S(1)} %get-tuple-element.22), channel_id=1, source_target_pairs={{0,4},{2,6},{4,0},{6,2},{8,12},{10,14},{12,8},{14,10},{1,5},{3,7},... | collective-permute-start | bytes 98312 | tf_op jit(solution)/shard_map/ppermute | solution.py:200
  43.3 1.1 %collective-permute-start.11 = (bf16[32,512]{1,0:T(8,128)(2,1)S(1)}, bf16[32,512]{1,0:T(8,128)(2,1)S(1)}, u32[]{:S(2)}, u32[]{:S(2)}) collective-permute-start(bf16[32,512]{1,0:T(8,128)(2,1)S(1)} %get-tuple-element.23), channel_id=1, source_target_pairs={{0,8},{2,10},{4,12},{6,14},{8,0},{10,2},{12,4},{14,6},{1,9},{3,11}... | collective-permute-start | bytes 98312 | tf_op jit(solution)/shard_map/ppermute | solution.py:200
  44.4 1.4 %collective-permute-start.12 = (bf16[32,512]{1,0:T(8,128)(2,1)S(1)}, bf16[32,512]{1,0:T(8,128)(2,1)S(1)}, u32[]{:S(2)}, u32[]{:S(2)}) collective-permute-start(bf16[32,512]{1,0:T(8,128)(2,1)S(1)} %get-tuple-element.24), channel_id=1, source_target_pairs={{0,12},{2,14},{4,8},{6,10},{8,4},{10,6},{12,0},{14,2},{1,13},{3,15... | collective-permute-start | bytes 98312 | tf_op jit(solution)/shard_map/ppermute | solution.py:200
  45.9 3.9 %collective-permute-start.17 = (bf16[64,2048]{1,0:T(8,128)(2,1)S(1)}, bf16[64,2048]{1,0:T(8,128)(2,1)S(1)}, u32[]{:S(2)}, u32[]{:S(2)}) collective-permute-start(bf16[64,2048]{1,0:T(8,128)(2,1)S(1)} %get-tuple-element.30), channel_id=1, source_target_pairs={{0,8},{1,0},{2,10},{3,2},{4,12},{5,4},{6,14},{7,6},{8,1},{9,9},{10... | collective-permute-start | bytes 786440 | tf_op jit(solution)/shard_map/ppermute | solution.py:261
  49.8 0.0 collective-permute-done.10
  49.8 2.3 %collective-permute-start.18 = (bf16[64,2048]{1,0:T(8,128)(2,1)S(1)}, bf16[64,2048]{1,0:T(8,128)(2,1)S(1)}, u32[]{:S(2)}, u32[]{:S(2)}) collective-permute-start(bf16[64,2048]{1,0:T(8,128)(2,1)S(1)} %get-tuple-element.29), channel_id=1, source_target_pairs={{0,8},{1,0},{2,10},{3,2},{4,12},{5,4},{6,14},{7,6},{8,1},{9,9},{10... | collective-permute-start | bytes 786440 | tf_op jit(solution)/shard_map/ppermute | solution.py:261
  52.2 0.0 collective-permute-done.11
  52.2 0.0 collective-permute-done.12
  52.3 0.1 collective-permute-start.13
  52.4 1.3 %collective-permute-done.17.refs_4_ = bf16[64,2048]{1,0:T(8,128)(2,1)S(1)} collective-permute-done((bf16[64,2048]{1,0:T(8,128)(2,1)S(1)}, bf16[64,2048]{1,0:T(8,128)(2,1)S(1)}, u32[]{:S(2)}, u32[]{:S(2)}) %collective-permute-start.17) | collective-permute-done | bytes 262176 | tf_op jit(solution)/shard_map/ppermute | solution.py:261
  53.7 0.7 collective-permute-start.19
  54.4 2.1 %collective-permute-done.18.refs_5_ = bf16[64,2048]{1,0:T(8,128)(2,1)S(1)} collective-permute-done((bf16[64,2048]{1,0:T(8,128)(2,1)S(1)}, bf16[64,2048]{1,0:T(8,128)(2,1)S(1)}, u32[]{:S(2)}, u32[]{:S(2)}) %collective-permute-start.18) | collective-permute-done | bytes 262176 | tf_op jit(solution)/shard_map/ppermute | solution.py:261
  56.5 0.7 collective-permute-start.20
  57.2 0.0 collective-permute-done.13
  57.2 1.6 %collective-permute-start.14 = (bf16[64,256]{1,0:T(8,128)(2,1)S(1)}, bf16[64,256]{1,0:T(8,128)(2,1)S(1)}, u32[]{:S(2)}, u32[]{:S(2)}) collective-permute-start(bf16[64,256]{1,0:T(8,128)(2,1)S(1)} %pad_maximum_fusion.refs_0_), channel_id=1, source_target_pairs={{0,2},{2,0},{4,6},{6,4},{8,10},{10,8},{12,14},{14,12},{1,3},{3,1},... | collective-permute-start | bytes 98312 | tf_op jit(solution)/shard_map/ppermute | solution.py:200
  58.8 6.5 %collective-permute-start.15 = (bf16[64,256]{1,0:T(8,128)(2,1)S(1)}, bf16[64,256]{1,0:T(8,128)(2,1)S(1)}, u32[]{:S(2)}, u32[]{:S(2)}) collective-permute-start(bf16[64,256]{1,0:T(8,128)(2,1)S(1)} %pad_maximum_fusion.refs_0_), channel_id=1, source_target_pairs={{0,4},{2,6},{4,0},{6,2},{8,12},{10,14},{12,8},{14,10},{1,5},{3,7},... | collective-permute-start | bytes 98312 | tf_op jit(solution)/shard_map/ppermute | solution.py:200
  65.4 0.0 collective-permute-done.19.refs_6_
  65.4 0.0 collective-permute-start.16
  65.4 0.1 pad_add_fusion.place
  65.4 0.0 collective-permute-done.20.refs_7_
  65.4 0.0 collective-permute-done.beside_rows
  65.4 0.0 collective-permute-done.14.refs_1_
  65.5 1.8 %collective-permute-done.15.refs_2_ = bf16[64,256]{1,0:T(8,128)(2,1)S(1)} collective-permute-done((bf16[64,256]{1,0:T(8,128)(2,1)S(1)}, bf16[64,256]{1,0:T(8,128)(2,1)S(1)}, u32[]{:S(2)}, u32[]{:S(2)}) %collective-permute-start.15) | collective-permute-done | bytes 32800 | tf_op jit(solution)/shard_map/ppermute | solution.py:200
  67.2 3.1 %collective-permute-done.16.refs_3_ = bf16[64,256]{1,0:T(8,128)(2,1)S(1)} collective-permute-done((bf16[64,256]{1,0:T(8,128)(2,1)S(1)}, bf16[64,256]{1,0:T(8,128)(2,1)S(1)}, u32[]{:S(2)}, u32[]{:S(2)}) %collective-permute-start.16) | collective-permute-done | bytes 32800 | tf_op jit(solution)/shard_map/ppermute | solution.py:200
  70.3 1.1 %mixed_blocks.1 = (bf16[64,2048]{1,0:T(8,128)(2,1)S(1)}, bf16[64,2048]{1,0:T(8,128)(2,1)S(1)}, bf16[64,2048]{1,0:T(8,128)(2,1)S(1)}, bf16[64,2048]{1,0:T(8,128)(2,1)S(1)}) custom-call(s32[3]{0:T(128)S(1)} %pad_add_fusion.place, bf16[128,2048]{1,0:T(8,128)(2,1)S(1)} %copy-done, bf16[128,2048]{1,0:T(8,128)(2,1)S(1)} %collective-permute-done.beside_rows, ...), custom_call_target="tpu_custom_call" | custom-call | tf_op jit(solution)/shard_map/mixed_blocks/pallas_call | solution.py:158
  71.4 0.5 collective-permute-start.21
  71.8 0.4 collective-permute-start.22
  72.2 2.7 %collective-permute-start.23 = (bf16[64,2048]{1,0:T(8,128)(2,1)S(1)}, bf16[64,2048]{1,0:T(8,128)(2,1)S(1)}, u32[]{:S(2)}, u32[]{:S(2)}) collective-permute-start(bf16[64,2048]{1,0:T(8,128)(2,1)S(1)} %get-tuple-element.28), channel_id=1, source_target_pairs={{0,6},{2,4},{4,2},{6,0},{8,14},{10,12},{12,10},{14,8},{1,7},{3,5},... | collective-permute-start | bytes 786440 | tf_op jit(solution)/shard_map/ppermute | solution.py:200
  74.9 5.4 %collective-permute-done.21.refs_1_ = bf16[64,2048]{1,0:T(8,128)(2,1)S(1)} collective-permute-done((bf16[64,2048]{1,0:T(8,128)(2,1)S(1)}, bf16[64,2048]{1,0:T(8,128)(2,1)S(1)}, u32[]{:S(2)}, u32[]{:S(2)}) %collective-permute-start.21) | collective-permute-done | bytes 262176 | tf_op jit(solution)/shard_map/ppermute | solution.py:200
  80.4 0.3 collective-permute-done.22.refs_2_
  80.7 6.5 %collective-permute-done.23.refs_3_ = bf16[64,2048]{1,0:T(8,128)(2,1)S(1)} collective-permute-done((bf16[64,2048]{1,0:T(8,128)(2,1)S(1)}, bf16[64,2048]{1,0:T(8,128)(2,1)S(1)}, u32[]{:S(2)}, u32[]{:S(2)}) %collective-permute-start.23) | collective-permute-done | bytes 262176 | tf_op jit(solution)/shard_map/ppermute | solution.py:200
  87.2 1.0 %place.1 = bf16[64,8192]{1,0:T(8,128)(2,1)} custom-call(s32[1]{0:T(128)} %bitcast.index, bf16[64,2048]{1,0:T(8,128)(2,1)S(1)} %get-tuple-element.25.refs_0_, bf16[64,2048]{1,0:T(8,128)(2,1)S(1)} %collective-permute-done.21.refs_1_, bf16[64,2048]{1,0:T(8,128)(2,1)S(1)} %collective-permute-done.22.refs_2_, bf16[64,2048]{1,0:T(8,128)(2,1)S(1)} %collective-permute-done.23.refs_3_), custom_call_target="tpu_custom_call" | custom-call | tf_op jit(solution)/shard_map/place/pallas_call | solution.py:114
  (7 shorter events, 0.1 us)
Async XLA Ops:
  0.0 37.3 %copy-start = (bf16[128,2048]{1,0:T(8,128)(2,1)S(1)}, bf16[128,2048]{1,0:T(8,128)(2,1)}, u32[]{:S(2)}) copy-start(bf16[128,2048]{1,0:T(8,128)(2,1)} %own_rows.1) | copy-start | bytes 1572868
  0.0 19.1 %collective-permute-start.6 = (bf16[2048,128]{1,0:T(8,128)(2,1)}, bf16[2048,128]{1,0:T(8,128)(2,1)S(1)}, u32[]{:S(2)}, u32[]{:S(2)}) collective-permute-start(bf16[2048,128]{1,0:T(8,128)(2,1)} %refs_4_.1), channel_id=1, source_target_pairs={{0,2},{2,0},{4,6},{6,4},{8,10},{10,8},{12,14},{14,12},{1,3},{3,1},... | collective-permute-start | bytes 1572872 | tf_op jit(solution)/shard_map/ppermute | solution.py:200
  3.0 23.4 %collective-permute-start.8 = (bf16[2048,128]{1,0:T(8,128)(2,1)}, bf16[2048,128]{1,0:T(8,128)(2,1)S(1)}, u32[]{:S(2)}, u32[]{:S(2)}) collective-permute-start(bf16[2048,128]{1,0:T(8,128)(2,1)} %refs_6_.1), channel_id=1, source_target_pairs={{0,2},{2,0},{4,6},{6,4},{8,10},{10,8},{12,14},{14,12},{1,3},{3,1},... | collective-permute-start | bytes 1572872 | tf_op jit(solution)/shard_map/ppermute | solution.py:200
  3.1 1.6 %copy-start.1 = (bf16[64,16384]{1,0:T(8,128)(2,1)S(1)}, bf16[64,16384]{1,0:T(8,128)(2,1)}, u32[]{:S(2)}) copy-start(bf16[64,16384]{1,0:T(8,128)(2,1)} %tokens.1) | copy-start | bytes 6291460
  4.7 5.7 %copy-start.2 = (bf16[2048,128]{1,0:T(8,128)(2,1)S(1)}, bf16[2048,128]{1,0:T(8,128)(2,1)}, u32[]{:S(2)}) copy-start(bf16[2048,128]{1,0:T(8,128)(2,1)} %refs_4_.1) | copy-start | bytes 1572868
  4.7 14.3 %copy-start.3 = (bf16[2048,128]{1,0:T(8,128)(2,1)S(1)}, bf16[2048,128]{1,0:T(8,128)(2,1)}, u32[]{:S(2)}) copy-start(bf16[2048,128]{1,0:T(8,128)(2,1)} %refs_6_.1) | copy-start | bytes 1572868
  5.7 13.4 %collective-permute-start.1 = (bf16[32,4096]{1,0:T(8,128)(2,1)S(1)}, bf16[32,4096]{1,0:T(8,128)(2,1)S(1)}, u32[]{:S(2)}, u32[]{:S(2)}) collective-permute-start(bf16[32,4096]{1,0:T(8,128)(2,1)S(1)} %get-tuple-element.18), channel_id=1, source_target_pairs={{0,4},{2,6},{4,0},{6,2},{8,12},{10,14},{12,8},{14,10},{1,5},{3,7},... | collective-permute-start | bytes 786440 | tf_op jit(solution)/shard_map/ppermute | solution.py:200
  7.8 18.5 %collective-permute-start.2 = (bf16[32,4096]{1,0:T(8,128)(2,1)S(1)}, bf16[32,4096]{1,0:T(8,128)(2,1)S(1)}, u32[]{:S(2)}, u32[]{:S(2)}) collective-permute-start(bf16[32,4096]{1,0:T(8,128)(2,1)S(1)} %get-tuple-element.19), channel_id=1, source_target_pairs={{0,8},{2,10},{4,12},{6,14},{8,0},{10,2},{12,4},{14,6},{1,9},{3,11}... | collective-permute-start | bytes 786440 | tf_op jit(solution)/shard_map/ppermute | solution.py:200
  10.4 26.9 %collective-permute-start.4 = (bf16[2048,128]{1,0:T(8,128)(2,1)S(1)}, bf16[2048,128]{1,0:T(8,128)(2,1)S(1)}, u32[]{:S(2)}, u32[]{:S(2)}) collective-permute-start(bf16[2048,128]{1,0:T(8,128)(2,1)S(1)} %copy-done.2), channel_id=1, source_target_pairs={{0,1},{1,0},{2,3},{3,2},{4,5},{5,4},{6,7},{7,6},{8,9},{9,8},{10,11... | collective-permute-start | bytes 1572872 | tf_op jit(solution)/shard_map/ppermute | solution.py:204
  19.1 18.2 %collective-permute-start.5 = (bf16[2048,128]{1,0:T(8,128)(2,1)S(1)}, bf16[2048,128]{1,0:T(8,128)(2,1)S(1)}, u32[]{:S(2)}, u32[]{:S(2)}) collective-permute-start(bf16[2048,128]{1,0:T(8,128)(2,1)S(1)} %copy-done.3), channel_id=1, source_target_pairs={{0,1},{1,0},{2,3},{3,2},{4,5},{5,4},{6,7},{7,6},{8,9},{9,8},{10,11... | collective-permute-start | bytes 1572872 | tf_op jit(solution)/shard_map/ppermute | solution.py:204
  19.1 18.2 %collective-permute-start.7 = (bf16[2048,128]{1,0:T(8,128)(2,1)S(1)}, bf16[2048,128]{1,0:T(8,128)(2,1)S(1)}, u32[]{:S(2)}, u32[]{:S(2)}) collective-permute-start(bf16[2048,128]{1,0:T(8,128)(2,1)S(1)} %collective-permute-done.6.refs_8_), channel_id=1, source_target_pairs={{0,1},{1,0},{2,3},{3,2},{4,5},{5,4},{6,7},{7,6},{8,9},{9,8},{10,11... | collective-permute-start | bytes 1572872 | tf_op jit(solution)/shard_map/ppermute | solution.py:204
  26.3 11.0 %collective-permute-start.9 = (bf16[2048,128]{1,0:T(8,128)(2,1)S(1)}, bf16[2048,128]{1,0:T(8,128)(2,1)S(1)}, u32[]{:S(2)}, u32[]{:S(2)}) collective-permute-start(bf16[2048,128]{1,0:T(8,128)(2,1)S(1)} %collective-permute-done.8.refs_10_), channel_id=1, source_target_pairs={{0,1},{1,0},{2,3},{3,2},{4,5},{5,4},{6,7},{7,6},{8,9},{9,8},{10,11... | collective-permute-start | bytes 1572872 | tf_op jit(solution)/shard_map/ppermute | solution.py:204
  26.3 10.9 %collective-permute-start.3 = (bf16[32,4096]{1,0:T(8,128)(2,1)S(1)}, bf16[32,4096]{1,0:T(8,128)(2,1)S(1)}, u32[]{:S(2)}, u32[]{:S(2)}) collective-permute-start(bf16[32,4096]{1,0:T(8,128)(2,1)S(1)} %get-tuple-element.20), channel_id=1, source_target_pairs={{0,12},{2,14},{4,8},{6,10},{8,4},{10,6},{12,0},{14,2},{1,13},{3,15... | collective-permute-start | bytes 786440 | tf_op jit(solution)/shard_map/ppermute | solution.py:200
  37.3 28.2 %collective-permute-start = (bf16[128,2048]{1,0:T(8,128)(2,1)S(1)}, bf16[128,2048]{1,0:T(8,128)(2,1)S(1)}, u32[]{:S(2)}, u32[]{:S(2)}) collective-permute-start(bf16[128,2048]{1,0:T(8,128)(2,1)S(1)} %copy-done), channel_id=1, source_target_pairs={{0,1},{1,0},{2,3},{3,2},{4,5},{5,4},{6,7},{7,6},{8,9},{9,8},{10,11... | collective-permute-start | bytes 1572872 | tf_op jit(solution)/shard_map/ppermute | solution.py:204
  38.0 11.8 %collective-permute-start.10 = (bf16[32,512]{1,0:T(8,128)(2,1)S(1)}, bf16[32,512]{1,0:T(8,128)(2,1)S(1)}, u32[]{:S(2)}, u32[]{:S(2)}) collective-permute-start(bf16[32,512]{1,0:T(8,128)(2,1)S(1)} %get-tuple-element.22), channel_id=1, source_target_pairs={{0,4},{2,6},{4,0},{6,2},{8,12},{10,14},{12,8},{14,10},{1,5},{3,7},... | collective-permute-start | bytes 98312 | tf_op jit(solution)/shard_map/ppermute | solution.py:200
  43.3 8.8 %collective-permute-start.11 = (bf16[32,512]{1,0:T(8,128)(2,1)S(1)}, bf16[32,512]{1,0:T(8,128)(2,1)S(1)}, u32[]{:S(2)}, u32[]{:S(2)}) collective-permute-start(bf16[32,512]{1,0:T(8,128)(2,1)S(1)} %get-tuple-element.23), channel_id=1, source_target_pairs={{0,8},{2,10},{4,12},{6,14},{8,0},{10,2},{12,4},{14,6},{1,9},{3,11}... | collective-permute-start | bytes 98312 | tf_op jit(solution)/shard_map/ppermute | solution.py:200
  44.4 7.8 %collective-permute-start.12 = (bf16[32,512]{1,0:T(8,128)(2,1)S(1)}, bf16[32,512]{1,0:T(8,128)(2,1)S(1)}, u32[]{:S(2)}, u32[]{:S(2)}) collective-permute-start(bf16[32,512]{1,0:T(8,128)(2,1)S(1)} %get-tuple-element.24), channel_id=1, source_target_pairs={{0,12},{2,14},{4,8},{6,10},{8,4},{10,6},{12,0},{14,2},{1,13},{3,15... | collective-permute-start | bytes 98312 | tf_op jit(solution)/shard_map/ppermute | solution.py:200
  45.9 7.9 %collective-permute-start.17 = (bf16[64,2048]{1,0:T(8,128)(2,1)S(1)}, bf16[64,2048]{1,0:T(8,128)(2,1)S(1)}, u32[]{:S(2)}, u32[]{:S(2)}) collective-permute-start(bf16[64,2048]{1,0:T(8,128)(2,1)S(1)} %get-tuple-element.30), channel_id=1, source_target_pairs={{0,8},{1,0},{2,10},{3,2},{4,12},{5,4},{6,14},{7,6},{8,1},{9,9},{10... | collective-permute-start | bytes 786440 | tf_op jit(solution)/shard_map/ppermute | solution.py:261
  49.8 6.7 %collective-permute-start.18 = (bf16[64,2048]{1,0:T(8,128)(2,1)S(1)}, bf16[64,2048]{1,0:T(8,128)(2,1)S(1)}, u32[]{:S(2)}, u32[]{:S(2)}) collective-permute-start(bf16[64,2048]{1,0:T(8,128)(2,1)S(1)} %get-tuple-element.29), channel_id=1, source_target_pairs={{0,8},{1,0},{2,10},{3,2},{4,12},{5,4},{6,14},{7,6},{8,1},{9,9},{10... | collective-permute-start | bytes 786440 | tf_op jit(solution)/shard_map/ppermute | solution.py:261
  52.3 4.9 %collective-permute-start.13 = (bf16[32,256]{1,0:T(8,128)(2,1)S(1)}, bf16[32,256]{1,0:T(8,128)(2,1)S(1)}, u32[]{:S(2)}, u32[]{:S(2)}) collective-permute-start(bf16[32,256]{1,0:T(8,128)(2,1)S(1)} %pad_maximum_fusion.1), channel_id=1, source_target_pairs={{0,1},{1,0},{2,3},{3,2},{4,5},{5,4},{6,7},{7,6},{8,9},{9,8},{10,11... | collective-permute-start | bytes 49160 | tf_op jit(solution)/shard_map/ppermute | solution.py:204
  53.7 11.6 %collective-permute-start.19 = (bf16[64,2048]{1,0:T(8,128)(2,1)S(1)}, bf16[64,2048]{1,0:T(8,128)(2,1)S(1)}, u32[]{:S(2)}, u32[]{:S(2)}) collective-permute-start(bf16[64,2048]{1,0:T(8,128)(2,1)S(1)} %collective-permute-done.17.refs_4_), channel_id=1, source_target_pairs={{0,0},{1,17},{2,2},{3,19},{4,4},{5,21},{6,6},{7,23},{8,24},{9,9},{... | collective-permute-start | bytes 786440 | tf_op jit(solution)/shard_map/ppermute | solution.py:263
  56.5 8.9 %collective-permute-start.20 = (bf16[64,2048]{1,0:T(8,128)(2,1)S(1)}, bf16[64,2048]{1,0:T(8,128)(2,1)S(1)}, u32[]{:S(2)}, u32[]{:S(2)}) collective-permute-start(bf16[64,2048]{1,0:T(8,128)(2,1)S(1)} %collective-permute-done.18.refs_5_), channel_id=1, source_target_pairs={{0,0},{1,17},{2,2},{3,19},{4,4},{5,21},{6,6},{7,23},{8,24},{9,9},{... | collective-permute-start | bytes 786440 | tf_op jit(solution)/shard_map/ppermute | solution.py:263
  57.2 8.2 %collective-permute-start.14 = (bf16[64,256]{1,0:T(8,128)(2,1)S(1)}, bf16[64,256]{1,0:T(8,128)(2,1)S(1)}, u32[]{:S(2)}, u32[]{:S(2)}) collective-permute-start(bf16[64,256]{1,0:T(8,128)(2,1)S(1)} %pad_maximum_fusion.refs_0_), channel_id=1, source_target_pairs={{0,2},{2,0},{4,6},{6,4},{8,10},{10,8},{12,14},{14,12},{1,3},{3,1},... | collective-permute-start | bytes 98312 | tf_op jit(solution)/shard_map/ppermute | solution.py:200
  58.8 8.4 %collective-permute-start.15 = (bf16[64,256]{1,0:T(8,128)(2,1)S(1)}, bf16[64,256]{1,0:T(8,128)(2,1)S(1)}, u32[]{:S(2)}, u32[]{:S(2)}) collective-permute-start(bf16[64,256]{1,0:T(8,128)(2,1)S(1)} %pad_maximum_fusion.refs_0_), channel_id=1, source_target_pairs={{0,4},{2,6},{4,0},{6,2},{8,12},{10,14},{12,8},{14,10},{1,5},{3,7},... | collective-permute-start | bytes 98312 | tf_op jit(solution)/shard_map/ppermute | solution.py:200
  65.4 5.0 %collective-permute-start.16 = (bf16[64,256]{1,0:T(8,128)(2,1)S(1)}, bf16[64,256]{1,0:T(8,128)(2,1)S(1)}, u32[]{:S(2)}, u32[]{:S(2)}) collective-permute-start(bf16[64,256]{1,0:T(8,128)(2,1)S(1)} %pad_maximum_fusion.refs_0_), channel_id=1, source_target_pairs={{0,6},{2,4},{4,2},{6,0},{8,14},{10,12},{12,10},{14,8},{1,7},{3,5},... | collective-permute-start | bytes 98312 | tf_op jit(solution)/shard_map/ppermute | solution.py:200
  71.4 9.0 %collective-permute-start.21 = (bf16[64,2048]{1,0:T(8,128)(2,1)S(1)}, bf16[64,2048]{1,0:T(8,128)(2,1)S(1)}, u32[]{:S(2)}, u32[]{:S(2)}) collective-permute-start(bf16[64,2048]{1,0:T(8,128)(2,1)S(1)} %get-tuple-element.26), channel_id=1, source_target_pairs={{0,2},{2,0},{4,6},{6,4},{8,10},{10,8},{12,14},{14,12},{1,3},{3,1},... | collective-permute-start | bytes 786440 | tf_op jit(solution)/shard_map/ppermute | solution.py:200
  71.8 8.9 %collective-permute-start.22 = (bf16[64,2048]{1,0:T(8,128)(2,1)S(1)}, bf16[64,2048]{1,0:T(8,128)(2,1)S(1)}, u32[]{:S(2)}, u32[]{:S(2)}) collective-permute-start(bf16[64,2048]{1,0:T(8,128)(2,1)S(1)} %get-tuple-element.27), channel_id=1, source_target_pairs={{0,4},{2,6},{4,0},{6,2},{8,12},{10,14},{12,8},{14,10},{1,5},{3,7},... | collective-permute-start | bytes 786440 | tf_op jit(solution)/shard_map/ppermute | solution.py:200
  72.2 15.0 %collective-permute-start.23 = (bf16[64,2048]{1,0:T(8,128)(2,1)S(1)}, bf16[64,2048]{1,0:T(8,128)(2,1)S(1)}, u32[]{:S(2)}, u32[]{:S(2)}) collective-permute-start(bf16[64,2048]{1,0:T(8,128)(2,1)S(1)} %get-tuple-element.28), channel_id=1, source_target_pairs={{0,6},{2,4},{4,2},{6,0},{8,14},{10,12},{12,10},{14,8},{1,7},{3,5},... | collective-permute-start | bytes 786440 | tf_op jit(solution)/shard_map/ppermute | solution.py:200

commit v4 on v3

--- a/solution.py
+++ b/solution.py
@@ -124,43 +124,44 @@
 
 def mixed_kernel(place, own_rows, beside_rows, *refs, n_hidden, n_far):
     hidden, far = refs[:n_hidden], refs[n_hidden : n_hidden + 2 * n_far]
-    outs, down = refs[n_hidden + 2 * n_far : -1], refs[-1]
+    outs = refs[n_hidden + 2 * n_far :]
     rows = hidden[0].shape[0]
     units = own_rows.shape[0]
     own, core, group = place[0], place[1], place[2]
 
+    stacked = jnp.concatenate([h[...] for h in hidden], axis=0)
+
+    def give(index, first, second):
+        low, high = stacked[:, :units], stacked[:, units:]
+        result = jnp.dot(
+            jnp.where(index == 0, low, high), first, preferred_element_type=jnp.float32
+        ) + jnp.dot(jnp.where(index == 0, high, low), second, preferred_element_type=jnp.float32)
+        for k, out in enumerate(outs):
+            out[...] = result[k * rows : (k + 1) * rows].astype(out.dtype)
+
     @pl.when(own == 1)
     def _():
-        down[pl.ds(pl.multiple_of(core * units, units), units)] = own_rows[...]
-        down[pl.ds(pl.multiple_of((1 - core) * units, units), units)] = beside_rows[...]
+        give(core, own_rows[...], beside_rows[...])
 
     @pl.when(own != 1)
     def _():
-        size = units // n_far
-        for k, piece in enumerate(far):
-            of = group if k < n_far else 1 - group
-            first = pl.multiple_of(of * units + k % n_far * size, size)
-            down[pl.ds(first, size)] = piece[...]
-
-    result = jnp.dot(
-        jnp.concatenate([h[...] for h in hidden], axis=0),
-        down[...],
-        preferred_element_type=jnp.float32,
-    )
-    for k, out in enumerate(outs):
-        out[...] = result[k * rows : (k + 1) * rows].astype(out.dtype)
+        pieces = [piece[...] for piece in far]
+        give(
+            group,
+            jnp.concatenate(pieces[:n_far], axis=0),
+            jnp.concatenate(pieces[n_far:], axis=0),
+        )
 
 
 def mixed_blocks(place, own_rows, beside_rows, hidden, far):
     rows = hidden[0].shape[0]
-    units, columns = own_rows.shape
+    _, columns = own_rows.shape
     vmem = pl.BlockSpec(memory_space=pltpu.VMEM)
     return pl.pallas_call(
         functools.partial(mixed_kernel, n_hidden=len(hidden), n_far=len(far) // 2),
         out_shape=[jax.ShapeDtypeStruct((rows, columns), jnp.bfloat16)] * len(hidden),
         in_specs=[pl.BlockSpec(memory_space=pltpu.SMEM)] + [vmem] * (2 + len(hidden) + len(far)),
         out_specs=[vmem] * len(hidden),
-        scratch_shapes=[pltpu.VMEM((2 * units, columns), jnp.bfloat16)],
         compiler_params=pltpu.CompilerParams(vmem_limit_bytes=16 * 1024 * 1024),
         name="mixed_blocks",
     )(place, own_rows, beside_rows, *hidden, *far)

time: 88.4 us -> 88.6 us (level)
  no operation moved by 1% of the time
where the time goes in v4:
time: 88.6 us; the launch traced here: 88.3 us
  waiting for transfers between devices  43.1 us (49%)
  starting transfers between devices  39.3 us (44%)
  Pallas kernels  3.92 us (4%)
  local copies, waits for them, and re-layouts  1.73 us (2%)
    ppermute x14, waiting for transfers between devices, away(): return lax.ppermute(value, 'batch', [(b, b ^ step) for b in range(n_batch)])  39.6 us
    ppermute x14, starting transfers between devices, away(): return lax.ppermute(value, 'batch', [(b, b ^ step) for b in range(n_batch)])  31 us
    ppermute x2, starting transfers between devices, halved_plan(): far.append(lax.ppermute(rows_of, wide, fetch))  6.28 us
    ppermute x2, waiting for transfers between devices, halved_plan(): far.append(lax.ppermute(rows_of, wide, fetch))  3.44 us
  transfers between devices with their start and end apart: 24, of which 10 were waited for; matrix products, arithmetic and copies ran while one was open for 0% of the time, Pallas kernels for 2%

profile of v4, /device:TPU:0, one launch (start us, length us, event | category | flops | bytes accessed | tf_op | source)
XLA Modules:
  0.0 88.3 jit_solution(16205230286853303956)
XLA Ops:
  0.0 0.0 copy-start
  0.0 3.0 %collective-permute-start.6 = (bf16[2048,128]{1,0:T(8,128)(2,1)}, bf16[2048,128]{1,0:T(8,128)(2,1)S(1)}, u32[]{:S(2)}, u32[]{:S(2)}) collective-permute-start(bf16[2048,128]{1,0:T(8,128)(2,1)} %refs_4_.1), channel_id=1, source_target_pairs={{0,2},{2,0},{4,6},{6,4},{8,10},{10,8},{12,14},{14,12},{1,3},{3,1},... | collective-permute-start | bytes 1572872 | tf_op jit(solution)/shard_map/ppermute | solution.py:201
  3.0 0.1 collective-permute-start.8
  3.0 0.1 stack.59.place
  3.1 0.0 copy-start.1
  3.1 1.6 %copy-done.1 = bf16[64,16384]{1,0:T(8,128)(2,1)S(1)} copy-done((bf16[64,16384]{1,0:T(8,128)(2,1)S(1)}, bf16[64,16384]{1,0:T(8,128)(2,1)}, u32[]{:S(2)}) %copy-start.1) | copy-done | bytes 2097176
  4.7 0.0 copy-start.2
  4.7 0.0 copy-start.3
  4.7 1.0 %cut.1 = (bf16[32,4096]{1,0:T(8,128)(2,1)S(1)}, bf16[32,4096]{1,0:T(8,128)(2,1)S(1)}, bf16[32,4096]{1,0:T(8,128)(2,1)S(1)}, bf16[32,4096]{1,0:T(8,128)(2,1)S(1)}) custom-call(s32[9]{0:T(128)S(1)} %stack.59.place, bf16[64,16384]{1,0:T(8,128)(2,1)S(1)} %copy-done.1), custom_call_target="tpu_custom_call" | custom-call | tf_op jit(solution)/shard_map/cut/pallas_call | solution.py:45
  5.7 2.1 %collective-permute-start.1 = (bf16[32,4096]{1,0:T(8,128)(2,1)S(1)}, bf16[32,4096]{1,0:T(8,128)(2,1)S(1)}, u32[]{:S(2)}, u32[]{:S(2)}) collective-permute-start(bf16[32,4096]{1,0:T(8,128)(2,1)S(1)} %get-tuple-element.18), channel_id=1, source_target_pairs={{0,4},{2,6},{4,0},{6,2},{8,12},{10,14},{12,8},{14,10},{1,5},{3,7},... | collective-permute-start | bytes 786440 | tf_op jit(solution)/shard_map/ppermute | solution.py:201
  7.8 2.6 %collective-permute-start.2 = (bf16[32,4096]{1,0:T(8,128)(2,1)S(1)}, bf16[32,4096]{1,0:T(8,128)(2,1)S(1)}, u32[]{:S(2)}, u32[]{:S(2)}) collective-permute-start(bf16[32,4096]{1,0:T(8,128)(2,1)S(1)} %get-tuple-element.19), channel_id=1, source_target_pairs={{0,8},{2,10},{4,12},{6,14},{8,0},{10,2},{12,4},{14,6},{1,9},{3,11}... | collective-permute-start | bytes 786440 | tf_op jit(solution)/shard_map/ppermute | solution.py:201
  10.4 0.0 copy-done.2
  10.4 0.0 collective-permute-start.4
  10.4 8.7 %collective-permute-done.1.refs_1_ = bf16[32,4096]{1,0:T(8,128)(2,1)S(1)} collective-permute-done((bf16[32,4096]{1,0:T(8,128)(2,1)S(1)}, bf16[32,4096]{1,0:T(8,128)(2,1)S(1)}, u32[]{:S(2)}, u32[]{:S(2)}) %collective-permute-start.1) | collective-permute-done | bytes 262176 | tf_op jit(solution)/shard_map/ppermute | solution.py:201
  19.1 0.0 copy-done.3
  19.1 0.0 collective-permute-start.5
  19.1 0.0 collective-permute-done.6.refs_8_
  19.1 0.5 collective-permute-start.7
  19.6 6.8 %collective-permute-done.8.refs_10_ = bf16[2048,128]{1,0:T(8,128)(2,1)S(1)} collective-permute-done((bf16[2048,128]{1,0:T(8,128)(2,1)}, bf16[2048,128]{1,0:T(8,128)(2,1)S(1)}, u32[]{:S(2)}, u32[]{:S(2)}) %collective-permute-start.8) | collective-permute-done | bytes 524320 | tf_op jit(solution)/shard_map/ppermute | solution.py:201
  26.3 0.0 collective-permute-start.9
  26.3 0.0 collective-permute-done.2.refs_2_
  26.3 3.9 %collective-permute-start.3 = (bf16[32,4096]{1,0:T(8,128)(2,1)S(1)}, bf16[32,4096]{1,0:T(8,128)(2,1)S(1)}, u32[]{:S(2)}, u32[]{:S(2)}) collective-permute-start(bf16[32,4096]{1,0:T(8,128)(2,1)S(1)} %get-tuple-element.20), channel_id=1, source_target_pairs={{0,12},{2,14},{4,8},{6,10},{8,4},{10,6},{12,0},{14,2},{1,13},{3,15... | collective-permute-start | bytes 786440 | tf_op jit(solution)/shard_map/ppermute | solution.py:201
  30.2 7.1 %collective-permute-done.3.refs_3_ = bf16[32,4096]{1,0:T(8,128)(2,1)S(1)} collective-permute-done((bf16[32,4096]{1,0:T(8,128)(2,1)S(1)}, bf16[32,4096]{1,0:T(8,128)(2,1)S(1)}, u32[]{:S(2)}, u32[]{:S(2)}) %collective-permute-start.3) | collective-permute-done | bytes 262176 | tf_op jit(solution)/shard_map/ppermute | solution.py:201
  37.3 0.0 copy-done
  37.3 0.0 collective-permute-start
  37.3 0.0 collective-permute-done.4.refs_5_
  37.3 0.0 collective-permute-done.5.refs_7_
  37.3 0.0 collective-permute-done.7.refs_9_
  37.3 0.0 collective-permute-done.9.refs_11_
  37.3 0.7 slab_sums.1
  38.0 5.3 %collective-permute-start.10 = (bf16[32,512]{1,0:T(8,128)(2,1)S(1)}, bf16[32,512]{1,0:T(8,128)(2,1)S(1)}, u32[]{:S(2)}, u32[]{:S(2)}) collective-permute-start(bf16[32,512]{1,0:T(8,128)(2,1)S(1)} %get-tuple-element.22), channel_id=1, source_target_pairs={{0,4},{2,6},{4,0},{6,2},{8,12},{10,14},{12,8},{14,10},{1,5},{3,7},... | collective-permute-start | bytes 98312 | tf_op jit(solution)/shard_map/ppermute | solution.py:201
  43.3 1.1 %collective-permute-start.11 = (bf16[32,512]{1,0:T(8,128)(2,1)S(1)}, bf16[32,512]{1,0:T(8,128)(2,1)S(1)}, u32[]{:S(2)}, u32[]{:S(2)}) collective-permute-start(bf16[32,512]{1,0:T(8,128)(2,1)S(1)} %get-tuple-element.23), channel_id=1, source_target_pairs={{0,8},{2,10},{4,12},{6,14},{8,0},{10,2},{12,4},{14,6},{1,9},{3,11}... | collective-permute-start | bytes 98312 | tf_op jit(solution)/shard_map/ppermute | solution.py:201
  44.4 1.4 %collective-permute-start.12 = (bf16[32,512]{1,0:T(8,128)(2,1)S(1)}, bf16[32,512]{1,0:T(8,128)(2,1)S(1)}, u32[]{:S(2)}, u32[]{:S(2)}) collective-permute-start(bf16[32,512]{1,0:T(8,128)(2,1)S(1)} %get-tuple-element.24), channel_id=1, source_target_pairs={{0,12},{2,14},{4,8},{6,10},{8,4},{10,6},{12,0},{14,2},{1,13},{3,15... | collective-permute-start | bytes 98312 | tf_op jit(solution)/shard_map/ppermute | solution.py:201
  45.9 3.9 %collective-permute-start.17 = (bf16[64,2048]{1,0:T(8,128)(2,1)S(1)}, bf16[64,2048]{1,0:T(8,128)(2,1)S(1)}, u32[]{:S(2)}, u32[]{:S(2)}) collective-permute-start(bf16[64,2048]{1,0:T(8,128)(2,1)S(1)} %get-tuple-element.30), channel_id=1, source_target_pairs={{0,8},{1,0},{2,10},{3,2},{4,12},{5,4},{6,14},{7,6},{8,1},{9,9},{10... | collective-permute-start | bytes 786440 | tf_op jit(solution)/shard_map/ppermute | solution.py:262
  49.8 0.0 collective-permute-done.10
  49.8 2.3 %collective-permute-start.18 = (bf16[64,2048]{1,0:T(8,128)(2,1)S(1)}, bf16[64,2048]{1,0:T(8,128)(2,1)S(1)}, u32[]{:S(2)}, u32[]{:S(2)}) collective-permute-start(bf16[64,2048]{1,0:T(8,128)(2,1)S(1)} %get-tuple-element.29), channel_id=1, source_target_pairs={{0,8},{1,0},{2,10},{3,2},{4,12},{5,4},{6,14},{7,6},{8,1},{9,9},{10... | collective-permute-start | bytes 786440 | tf_op jit(solution)/shard_map/ppermute | solution.py:262
  52.2 0.0 collective-permute-done.11
  52.2 0.0 collective-permute-done.12
  52.3 0.1 collective-permute-start.13
  52.4 1.3 %collective-permute-done.17.refs_4_ = bf16[64,2048]{1,0:T(8,128)(2,1)S(1)} collective-permute-done((bf16[64,2048]{1,0:T(8,128)(2,1)S(1)}, bf16[64,2048]{1,0:T(8,128)(2,1)S(1)}, u32[]{:S(2)}, u32[]{:S(2)}) %collective-permute-start.17) | collective-permute-done | bytes 262176 | tf_op jit(solution)/shard_map/ppermute | solution.py:262
  53.7 0.7 collective-permute-start.19
  54.4 2.1 %collective-permute-done.18.refs_5_ = bf16[64,2048]{1,0:T(8,128)(2,1)S(1)} collective-permute-done((bf16[64,2048]{1,0:T(8,128)(2,1)S(1)}, bf16[64,2048]{1,0:T(8,128)(2,1)S(1)}, u32[]{:S(2)}, u32[]{:S(2)}) %collective-permute-start.18) | collective-permute-done | bytes 262176 | tf_op jit(solution)/shard_map/ppermute | solution.py:262
  56.5 0.7 collective-permute-start.20
  57.2 0.0 collective-permute-done.13
  57.2 1.6 %collective-permute-start.14 = (bf16[64,256]{1,0:T(8,128)(2,1)S(1)}, bf16[64,256]{1,0:T(8,128)(2,1)S(1)}, u32[]{:S(2)}, u32[]{:S(2)}) collective-permute-start(bf16[64,256]{1,0:T(8,128)(2,1)S(1)} %pad_maximum_fusion.refs_0_), channel_id=1, source_target_pairs={{0,2},{2,0},{4,6},{6,4},{8,10},{10,8},{12,14},{14,12},{1,3},{3,1},... | collective-permute-start | bytes 98312 | tf_op jit(solution)/shard_map/ppermute | solution.py:201
  58.8 6.5 %collective-permute-start.15 = (bf16[64,256]{1,0:T(8,128)(2,1)S(1)}, bf16[64,256]{1,0:T(8,128)(2,1)S(1)}, u32[]{:S(2)}, u32[]{:S(2)}) collective-permute-start(bf16[64,256]{1,0:T(8,128)(2,1)S(1)} %pad_maximum_fusion.refs_0_), channel_id=1, source_target_pairs={{0,4},{2,6},{4,0},{6,2},{8,12},{10,14},{12,8},{14,10},{1,5},{3,7},... | collective-permute-start | bytes 98312 | tf_op jit(solution)/shard_map/ppermute | solution.py:201
  65.4 0.0 collective-permute-done.19.refs_6_
  65.4 0.0 collective-permute-start.16
  65.4 0.1 pad_add_fusion.place
  65.4 0.0 collective-permute-done.20.refs_7_
  65.4 0.0 collective-permute-done.beside_rows
  65.4 0.0 collective-permute-done.14.refs_1_
  65.5 1.8 %collective-permute-done.15.refs_2_ = bf16[64,256]{1,0:T(8,128)(2,1)S(1)} collective-permute-done((bf16[64,256]{1,0:T(8,128)(2,1)S(1)}, bf16[64,256]{1,0:T(8,128)(2,1)S(1)}, u32[]{:S(2)}, u32[]{:S(2)}) %collective-permute-start.15) | collective-permute-done | bytes 32800 | tf_op jit(solution)/shard_map/ppermute | solution.py:201
  67.2 3.1 %collective-permute-done.16.refs_3_ = bf16[64,256]{1,0:T(8,128)(2,1)S(1)} collective-permute-done((bf16[64,256]{1,0:T(8,128)(2,1)S(1)}, bf16[64,256]{1,0:T(8,128)(2,1)S(1)}, u32[]{:S(2)}, u32[]{:S(2)}) %collective-permute-start.16) | collective-permute-done | bytes 32800 | tf_op jit(solution)/shard_map/ppermute | solution.py:201
  70.3 1.2 %mixed_blocks.1 = (bf16[64,2048]{1,0:T(8,128)(2,1)S(1)}, bf16[64,2048]{1,0:T(8,128)(2,1)S(1)}, bf16[64,2048]{1,0:T(8,128)(2,1)S(1)}, bf16[64,2048]{1,0:T(8,128)(2,1)S(1)}) custom-call(s32[3]{0:T(128)S(1)} %pad_add_fusion.place, bf16[128,2048]{1,0:T(8,128)(2,1)S(1)} %copy-done, bf16[128,2048]{1,0:T(8,128)(2,1)S(1)} %collective-permute-done.beside_rows, ...), custom_call_target="tpu_custom_call" | custom-call | tf_op jit(solution)/shard_map/mixed_blocks/pallas_call | solution.py:160
  71.6 0.5 collective-permute-start.21
  72.0 0.4 collective-permute-start.22
  72.4 2.7 %collective-permute-start.23 = (bf16[64,2048]{1,0:T(8,128)(2,1)S(1)}, bf16[64,2048]{1,0:T(8,128)(2,1)S(1)}, u32[]{:S(2)}, u32[]{:S(2)}) collective-permute-start(bf16[64,2048]{1,0:T(8,128)(2,1)S(1)} %get-tuple-element.28), channel_id=1, source_target_pairs={{0,6},{2,4},{4,2},{6,0},{8,14},{10,12},{12,10},{14,8},{1,7},{3,5},... | collective-permute-start | bytes 786440 | tf_op jit(solution)/shard_map/ppermute | solution.py:201
  75.1 5.4 %collective-permute-done.21.refs_1_ = bf16[64,2048]{1,0:T(8,128)(2,1)S(1)} collective-permute-done((bf16[64,2048]{1,0:T(8,128)(2,1)S(1)}, bf16[64,2048]{1,0:T(8,128)(2,1)S(1)}, u32[]{:S(2)}, u32[]{:S(2)}) %collective-permute-start.21) | collective-permute-done | bytes 262176 | tf_op jit(solution)/shard_map/ppermute | solution.py:201
  80.5 0.3 collective-permute-done.22.refs_2_
  80.9 6.5 %collective-permute-done.23.refs_3_ = bf16[64,2048]{1,0:T(8,128)(2,1)S(1)} collective-permute-done((bf16[64,2048]{1,0:T(8,128)(2,1)S(1)}, bf16[64,2048]{1,0:T(8,128)(2,1)S(1)}, u32[]{:S(2)}, u32[]{:S(2)}) %collective-permute-start.23) | collective-permute-done | bytes 262176 | tf_op jit(solution)/shard_map/ppermute | solution.py:201
  87.3 1.0 %place.1 = bf16[64,8192]{1,0:T(8,128)(2,1)} custom-call(s32[1]{0:T(128)} %bitcast.index, bf16[64,2048]{1,0:T(8,128)(2,1)S(1)} %get-tuple-element.25.refs_0_, bf16[64,2048]{1,0:T(8,128)(2,1)S(1)} %collective-permute-done.21.refs_1_, bf16[64,2048]{1,0:T(8,128)(2,1)S(1)} %collective-permute-done.22.refs_2_, bf16[64,2048]{1,0:T(8,128)(2,1)S(1)} %collective-permute-done.23.refs_3_), custom_call_target="tpu_custom_call" | custom-call | tf_op jit(solution)/shard_map/place/pallas_call | solution.py:114
  (7 shorter events, 0.1 us)
Async XLA Ops:
  0.0 37.3 %copy-start = (bf16[128,2048]{1,0:T(8,128)(2,1)S(1)}, bf16[128,2048]{1,0:T(8,128)(2,1)}, u32[]{:S(2)}) copy-start(bf16[128,2048]{1,0:T(8,128)(2,1)} %own_rows.1) | copy-start | bytes 1572868
  0.0 19.1 %collective-permute-start.6 = (bf16[2048,128]{1,0:T(8,128)(2,1)}, bf16[2048,128]{1,0:T(8,128)(2,1)S(1)}, u32[]{:S(2)}, u32[]{:S(2)}) collective-permute-start(bf16[2048,128]{1,0:T(8,128)(2,1)} %refs_4_.1), channel_id=1, source_target_pairs={{0,2},{2,0},{4,6},{6,4},{8,10},{10,8},{12,14},{14,12},{1,3},{3,1},... | collective-permute-start | bytes 1572872 | tf_op jit(solution)/shard_map/ppermute | solution.py:201
  3.0 23.4 %collective-permute-start.8 = (bf16[2048,128]{1,0:T(8,128)(2,1)}, bf16[2048,128]{1,0:T(8,128)(2,1)S(1)}, u32[]{:S(2)}, u32[]{:S(2)}) collective-permute-start(bf16[2048,128]{1,0:T(8,128)(2,1)} %refs_6_.1), channel_id=1, source_target_pairs={{0,2},{2,0},{4,6},{6,4},{8,10},{10,8},{12,14},{14,12},{1,3},{3,1},... | collective-permute-start | bytes 1572872 | tf_op jit(solution)/shard_map/ppermute | solution.py:201
  3.1 1.6 %copy-start.1 = (bf16[64,16384]{1,0:T(8,128)(2,1)S(1)}, bf16[64,16384]{1,0:T(8,128)(2,1)}, u32[]{:S(2)}) copy-start(bf16[64,16384]{1,0:T(8,128)(2,1)} %tokens.1) | copy-start | bytes 6291460
  4.7 5.7 %copy-start.2 = (bf16[2048,128]{1,0:T(8,128)(2,1)S(1)}, bf16[2048,128]{1,0:T(8,128)(2,1)}, u32[]{:S(2)}) copy-start(bf16[2048,128]{1,0:T(8,128)(2,1)} %refs_4_.1) | copy-start | bytes 1572868
  4.7 14.3 %copy-start.3 = (bf16[2048,128]{1,0:T(8,128)(2,1)S(1)}, bf16[2048,128]{1,0:T(8,128)(2,1)}, u32[]{:S(2)}) copy-start(bf16[2048,128]{1,0:T(8,128)(2,1)} %refs_6_.1) | copy-start | bytes 1572868
  5.7 13.4 %collective-permute-start.1 = (bf16[32,4096]{1,0:T(8,128)(2,1)S(1)}, bf16[32,4096]{1,0:T(8,128)(2,1)S(1)}, u32[]{:S(2)}, u32[]{:S(2)}) collective-permute-start(bf16[32,4096]{1,0:T(8,128)(2,1)S(1)} %get-tuple-element.18), channel_id=1, source_target_pairs={{0,4},{2,6},{4,0},{6,2},{8,12},{10,14},{12,8},{14,10},{1,5},{3,7},... | collective-permute-start | bytes 786440 | tf_op jit(solution)/shard_map/ppermute | solution.py:201
  7.8 18.5 %collective-permute-start.2 = (bf16[32,4096]{1,0:T(8,128)(2,1)S(1)}, bf16[32,4096]{1,0:T(8,128)(2,1)S(1)}, u32[]{:S(2)}, u32[]{:S(2)}) collective-permute-start(bf16[32,4096]{1,0:T(8,128)(2,1)S(1)} %get-tuple-element.19), channel_id=1, source_target_pairs={{0,8},{2,10},{4,12},{6,14},{8,0},{10,2},{12,4},{14,6},{1,9},{3,11}... | collective-permute-start | bytes 786440 | tf_op jit(solution)/shard_map/ppermute | solution.py:201
  10.4 26.9 %collective-permute-start.4 = (bf16[2048,128]{1,0:T(8,128)(2,1)S(1)}, bf16[2048,128]{1,0:T(8,128)(2,1)S(1)}, u32[]{:S(2)}, u32[]{:S(2)}) collective-permute-start(bf16[2048,128]{1,0:T(8,128)(2,1)S(1)} %copy-done.2), channel_id=1, source_target_pairs={{0,1},{1,0},{2,3},{3,2},{4,5},{5,4},{6,7},{7,6},{8,9},{9,8},{10,11... | collective-permute-start | bytes 1572872 | tf_op jit(solution)/shard_map/ppermute | solution.py:205
  19.1 18.2 %collective-permute-start.5 = (bf16[2048,128]{1,0:T(8,128)(2,1)S(1)}, bf16[2048,128]{1,0:T(8,128)(2,1)S(1)}, u32[]{:S(2)}, u32[]{:S(2)}) collective-permute-start(bf16[2048,128]{1,0:T(8,128)(2,1)S(1)} %copy-done.3), channel_id=1, source_target_pairs={{0,1},{1,0},{2,3},{3,2},{4,5},{5,4},{6,7},{7,6},{8,9},{9,8},{10,11... | collective-permute-start | bytes 1572872 | tf_op jit(solution)/shard_map/ppermute | solution.py:205
  19.1 18.2 %collective-permute-start.7 = (bf16[2048,128]{1,0:T(8,128)(2,1)S(1)}, bf16[2048,128]{1,0:T(8,128)(2,1)S(1)}, u32[]{:S(2)}, u32[]{:S(2)}) collective-permute-start(bf16[2048,128]{1,0:T(8,128)(2,1)S(1)} %collective-permute-done.6.refs_8_), channel_id=1, source_target_pairs={{0,1},{1,0},{2,3},{3,2},{4,5},{5,4},{6,7},{7,6},{8,9},{9,8},{10,11... | collective-permute-start | bytes 1572872 | tf_op jit(solution)/shard_map/ppermute | solution.py:205
  26.3 11.0 %collective-permute-start.9 = (bf16[2048,128]{1,0:T(8,128)(2,1)S(1)}, bf16[2048,128]{1,0:T(8,128)(2,1)S(1)}, u32[]{:S(2)}, u32[]{:S(2)}) collective-permute-start(bf16[2048,128]{1,0:T(8,128)(2,1)S(1)} %collective-permute-done.8.refs_10_), channel_id=1, source_target_pairs={{0,1},{1,0},{2,3},{3,2},{4,5},{5,4},{6,7},{7,6},{8,9},{9,8},{10,11... | collective-permute-start | bytes 1572872 | tf_op jit(solution)/shard_map/ppermute | solution.py:205
  26.3 10.9 %collective-permute-start.3 = (bf16[32,4096]{1,0:T(8,128)(2,1)S(1)}, bf16[32,4096]{1,0:T(8,128)(2,1)S(1)}, u32[]{:S(2)}, u32[]{:S(2)}) collective-permute-start(bf16[32,4096]{1,0:T(8,128)(2,1)S(1)} %get-tuple-element.20), channel_id=1, source_target_pairs={{0,12},{2,14},{4,8},{6,10},{8,4},{10,6},{12,0},{14,2},{1,13},{3,15... | collective-permute-start | bytes 786440 | tf_op jit(solution)/shard_map/ppermute | solution.py:201
  37.3 28.2 %collective-permute-start = (bf16[128,2048]{1,0:T(8,128)(2,1)S(1)}, bf16[128,2048]{1,0:T(8,128)(2,1)S(1)}, u32[]{:S(2)}, u32[]{:S(2)}) collective-permute-start(bf16[128,2048]{1,0:T(8,128)(2,1)S(1)} %copy-done), channel_id=1, source_target_pairs={{0,1},{1,0},{2,3},{3,2},{4,5},{5,4},{6,7},{7,6},{8,9},{9,8},{10,11... | collective-permute-start | bytes 1572872 | tf_op jit(solution)/shard_map/ppermute | solution.py:205
  38.0 11.8 %collective-permute-start.10 = (bf16[32,512]{1,0:T(8,128)(2,1)S(1)}, bf16[32,512]{1,0:T(8,128)(2,1)S(1)}, u32[]{:S(2)}, u32[]{:S(2)}) collective-permute-start(bf16[32,512]{1,0:T(8,128)(2,1)S(1)} %get-tuple-element.22), channel_id=1, source_target_pairs={{0,4},{2,6},{4,0},{6,2},{8,12},{10,14},{12,8},{14,10},{1,5},{3,7},... | collective-permute-start | bytes 98312 | tf_op jit(solution)/shard_map/ppermute | solution.py:201
  43.3 8.8 %collective-permute-start.11 = (bf16[32,512]{1,0:T(8,128)(2,1)S(1)}, bf16[32,512]{1,0:T(8,128)(2,1)S(1)}, u32[]{:S(2)}, u32[]{:S(2)}) collective-permute-start(bf16[32,512]{1,0:T(8,128)(2,1)S(1)} %get-tuple-element.23), channel_id=1, source_target_pairs={{0,8},{2,10},{4,12},{6,14},{8,0},{10,2},{12,4},{14,6},{1,9},{3,11}... | collective-permute-start | bytes 98312 | tf_op jit(solution)/shard_map/ppermute | solution.py:201
  44.4 7.8 %collective-permute-start.12 = (bf16[32,512]{1,0:T(8,128)(2,1)S(1)}, bf16[32,512]{1,0:T(8,128)(2,1)S(1)}, u32[]{:S(2)}, u32[]{:S(2)}) collective-permute-start(bf16[32,512]{1,0:T(8,128)(2,1)S(1)} %get-tuple-element.24), channel_id=1, source_target_pairs={{0,12},{2,14},{4,8},{6,10},{8,4},{10,6},{12,0},{14,2},{1,13},{3,15... | collective-permute-start | bytes 98312 | tf_op jit(solution)/shard_map/ppermute | solution.py:201
  45.9 7.9 %collective-permute-start.17 = (bf16[64,2048]{1,0:T(8,128)(2,1)S(1)}, bf16[64,2048]{1,0:T(8,128)(2,1)S(1)}, u32[]{:S(2)}, u32[]{:S(2)}) collective-permute-start(bf16[64,2048]{1,0:T(8,128)(2,1)S(1)} %get-tuple-element.30), channel_id=1, source_target_pairs={{0,8},{1,0},{2,10},{3,2},{4,12},{5,4},{6,14},{7,6},{8,1},{9,9},{10... | collective-permute-start | bytes 786440 | tf_op jit(solution)/shard_map/ppermute | solution.py:262
  49.8 6.7 %collective-permute-start.18 = (bf16[64,2048]{1,0:T(8,128)(2,1)S(1)}, bf16[64,2048]{1,0:T(8,128)(2,1)S(1)}, u32[]{:S(2)}, u32[]{:S(2)}) collective-permute-start(bf16[64,2048]{1,0:T(8,128)(2,1)S(1)} %get-tuple-element.29), channel_id=1, source_target_pairs={{0,8},{1,0},{2,10},{3,2},{4,12},{5,4},{6,14},{7,6},{8,1},{9,9},{10... | collective-permute-start | bytes 786440 | tf_op jit(solution)/shard_map/ppermute | solution.py:262
  52.3 4.9 %collective-permute-start.13 = (bf16[32,256]{1,0:T(8,128)(2,1)S(1)}, bf16[32,256]{1,0:T(8,128)(2,1)S(1)}, u32[]{:S(2)}, u32[]{:S(2)}) collective-permute-start(bf16[32,256]{1,0:T(8,128)(2,1)S(1)} %pad_maximum_fusion.1), channel_id=1, source_target_pairs={{0,1},{1,0},{2,3},{3,2},{4,5},{5,4},{6,7},{7,6},{8,9},{9,8},{10,11... | collective-permute-start | bytes 49160 | tf_op jit(solution)/shard_map/ppermute | solution.py:205
  53.7 11.6 %collective-permute-start.19 = (bf16[64,2048]{1,0:T(8,128)(2,1)S(1)}, bf16[64,2048]{1,0:T(8,128)(2,1)S(1)}, u32[]{:S(2)}, u32[]{:S(2)}) collective-permute-start(bf16[64,2048]{1,0:T(8,128)(2,1)S(1)} %collective-permute-done.17.refs_4_), channel_id=1, source_target_pairs={{0,0},{1,17},{2,2},{3,19},{4,4},{5,21},{6,6},{7,23},{8,24},{9,9},{... | collective-permute-start | bytes 786440 | tf_op jit(solution)/shard_map/ppermute | solution.py:264
  56.5 8.9 %collective-permute-start.20 = (bf16[64,2048]{1,0:T(8,128)(2,1)S(1)}, bf16[64,2048]{1,0:T(8,128)(2,1)S(1)}, u32[]{:S(2)}, u32[]{:S(2)}) collective-permute-start(bf16[64,2048]{1,0:T(8,128)(2,1)S(1)} %collective-permute-done.18.refs_5_), channel_id=1, source_target_pairs={{0,0},{1,17},{2,2},{3,19},{4,4},{5,21},{6,6},{7,23},{8,24},{9,9},{... | collective-permute-start | bytes 786440 | tf_op jit(solution)/shard_map/ppermute | solution.py:264
  57.2 8.2 %collective-permute-start.14 = (bf16[64,256]{1,0:T(8,128)(2,1)S(1)}, bf16[64,256]{1,0:T(8,128)(2,1)S(1)}, u32[]{:S(2)}, u32[]{:S(2)}) collective-permute-start(bf16[64,256]{1,0:T(8,128)(2,1)S(1)} %pad_maximum_fusion.refs_0_), channel_id=1, source_target_pairs={{0,2},{2,0},{4,6},{6,4},{8,10},{10,8},{12,14},{14,12},{1,3},{3,1},... | collective-permute-start | bytes 98312 | tf_op jit(solution)/shard_map/ppermute | solution.py:201
  58.8 8.4 %collective-permute-start.15 = (bf16[64,256]{1,0:T(8,128)(2,1)S(1)}, bf16[64,256]{1,0:T(8,128)(2,1)S(1)}, u32[]{:S(2)}, u32[]{:S(2)}) collective-permute-start(bf16[64,256]{1,0:T(8,128)(2,1)S(1)} %pad_maximum_fusion.refs_0_), channel_id=1, source_target_pairs={{0,4},{2,6},{4,0},{6,2},{8,12},{10,14},{12,8},{14,10},{1,5},{3,7},... | collective-permute-start | bytes 98312 | tf_op jit(solution)/shard_map/ppermute | solution.py:201
  65.4 5.0 %collective-permute-start.16 = (bf16[64,256]{1,0:T(8,128)(2,1)S(1)}, bf16[64,256]{1,0:T(8,128)(2,1)S(1)}, u32[]{:S(2)}, u32[]{:S(2)}) collective-permute-start(bf16[64,256]{1,0:T(8,128)(2,1)S(1)} %pad_maximum_fusion.refs_0_), channel_id=1, source_target_pairs={{0,6},{2,4},{4,2},{6,0},{8,14},{10,12},{12,10},{14,8},{1,7},{3,5},... | collective-permute-start | bytes 98312 | tf_op jit(solution)/shard_map/ppermute | solution.py:201
  71.6 9.0 %collective-permute-start.21 = (bf16[64,2048]{1,0:T(8,128)(2,1)S(1)}, bf16[64,2048]{1,0:T(8,128)(2,1)S(1)}, u32[]{:S(2)}, u32[]{:S(2)}) collective-permute-start(bf16[64,2048]{1,0:T(8,128)(2,1)S(1)} %get-tuple-element.26), channel_id=1, source_target_pairs={{0,2},{2,0},{4,6},{6,4},{8,10},{10,8},{12,14},{14,12},{1,3},{3,1},... | collective-permute-start | bytes 786440 | tf_op jit(solution)/shard_map/ppermute | solution.py:201
  72.0 8.9 %collective-permute-start.22 = (bf16[64,2048]{1,0:T(8,128)(2,1)S(1)}, bf16[64,2048]{1,0:T(8,128)(2,1)S(1)}, u32[]{:S(2)}, u32[]{:S(2)}) collective-permute-start(bf16[64,2048]{1,0:T(8,128)(2,1)S(1)} %get-tuple-element.27), channel_id=1, source_target_pairs={{0,4},{2,6},{4,0},{6,2},{8,12},{10,14},{12,8},{14,10},{1,5},{3,7},... | collective-permute-start | bytes 786440 | tf_op jit(solution)/shard_map/ppermute | solution.py:201
  72.4 15.0 %collective-permute-start.23 = (bf16[64,2048]{1,0:T(8,128)(2,1)S(1)}, bf16[64,2048]{1,0:T(8,128)(2,1)S(1)}, u32[]{:S(2)}, u32[]{:S(2)}) collective-permute-start(bf16[64,2048]{1,0:T(8,128)(2,1)S(1)} %get-tuple-element.28), channel_id=1, source_target_pairs={{0,6},{2,4},{4,2},{6,0},{8,14},{10,12},{12,10},{14,8},{1,7},{3,5},... | collective-permute-start | bytes 786440 | tf_op jit(solution)/shard_map/ppermute | solution.py:201
